TPU v7x, 32 devices: a whole 2x2x4 slice. The times are simulated.
32 devices in a mesh: groups: 1, fac: 32 (over z, y, x, core).
Axes of the slice: x: 2, y: 2, z: 4, core: 2. Of those that a mesh axis runs over, the one named last changes fastest.
Arguments:
- sky_image: float32 [64, 96, 4096], P(('groups', 'fac')), may hold values from 0 to 18, as said below
- measured_real: float32 [64, 96, 4096], P(('groups', 'fac')), may hold values from -6 to 6
- measured_imaginary: float32 [64, 96, 4096], P(('groups', 'fac')), may hold values from -6 to 6
- sampling_mask: int32 [64, 96, 4096], P(('groups', 'fac')), may hold values 0 or 1
- dual_field: float32 [64, 96, 4096], P('groups', None, 'fac'), may hold values from -6 to 6
Outputs:
- next_image: float32 [64, 96, 4096], P(('groups', 'fac'))
- next_dual: float32 [64, 96, 4096], P('groups', None, 'fac')
Inputs may be any that keep to these rules, and one draw needn't show every extreme that they name: `sky_image`: non-negative sky brightness.
All inputs are finite; a program needn't handle non-finite values. No bound on the sum of `sampling_mask` on one device may be relied on, other than what follows from the above.
Results may differ from a plain program's by a relative error of at most 0.00012.
Values sent between devices are 32-bit elements; how exact they have to be, the bound alone decides.
No kernel may reach another device: no remote copies, remote signals or barrier semaphores. Data moves between devices by JAX's collectives and lax.ppermute only.
A program may use at most 192 MiB of HBM per device.

v0:
```python
import jax
import jax.numpy as jnp
import numpy as np
from jax import lax
from jax.sharding import PartitionSpec as P

LEVELS = 4


low_pass = (
    0.2303778133088964,
    0.7148465705529155,
    0.6308807679298587,
    -0.0279837694168599,
    -0.1870348117190931,
    0.0308413818355607,
    0.0328830116668852,
    -0.010597401785069,
)
high_pass = tuple(((-1) ** tap_index * low_pass[7 - tap_index] for tap_index in range(8)))
primal_step = 0.6
dual_step = 0.8
ball_radius = 12.0
precise = lax.Precision.HIGHEST


def contract(pattern, left_side, right_side):
    return jnp.einsum(
        pattern, left_side, right_side, precision=precise, preferred_element_type=jnp.float32
    )


def fourier_table(length, direction):
    sample_grid = np.arange(length)
    angles = 2.0 * np.pi * (np.outer(sample_grid, sample_grid) % length) / length
    factor = 1.0 / np.sqrt(length)
    return (
        jnp.asarray(np.cos(angles) * factor, jnp.float32),
        jnp.asarray(direction * np.sin(angles) * factor, jnp.float32),
    )


def twist_table(inner_size, outer_size, length, direction):
    angles = (
        2.0
        * np.pi
        * (np.arange(inner_size)[:, None] * np.arange(outer_size)[None, :] % length)
        / length
    )
    return (
        jnp.asarray(np.cos(angles), jnp.float32),
        jnp.asarray(direction * np.sin(angles), jnp.float32),
    )


def complex_step(real_part, imag_part, pattern, matrix):
    if imag_part is None:
        return (contract(pattern, real_part, matrix[0]), contract(pattern, real_part, matrix[1]))
    return (
        contract(pattern, real_part, matrix[0]) - contract(pattern, imag_part, matrix[1]),
        contract(pattern, real_part, matrix[1]) + contract(pattern, imag_part, matrix[0]),
    )


def data_gradient(sky_image, measured_real, measured_imaginary, sampling_mask):
    channels, row_count, column_count = sky_image.shape
    outer_size = 64
    inner_size = column_count // outer_size
    sample_grid = sky_image.reshape(channels, row_count, inner_size, outer_size)
    real_part, imag_part = complex_step(
        sample_grid, None, "crba,rs->csba", fourier_table(row_count, -1.0)
    )
    real_part, imag_part = complex_step(
        real_part, imag_part, "csba,bk->cska", fourier_table(inner_size, -1.0)
    )
    twist_real, twist_imag = twist_table(inner_size, outer_size, column_count, -1.0)
    real_part, imag_part = (
        real_part * twist_real - imag_part * twist_imag,
        real_part * twist_imag + imag_part * twist_real,
    )
    real_part, imag_part = complex_step(
        real_part, imag_part, "cska,aj->csjk", fourier_table(outer_size, -1.0)
    )
    weights = sampling_mask.astype(jnp.float32)
    real_part = weights * (real_part.reshape(channels, row_count, column_count) - measured_real)
    imag_part = weights * (
        imag_part.reshape(channels, row_count, column_count) - measured_imaginary
    )
    real_part = real_part.reshape(channels, row_count, outer_size, inner_size)
    imag_part = imag_part.reshape(channels, row_count, outer_size, inner_size)
    real_part, imag_part = complex_step(
        real_part, imag_part, "csjk,ja->cska", fourier_table(outer_size, 1.0)
    )
    twist_real, twist_imag = twist_table(inner_size, outer_size, column_count, 1.0)
    real_part, imag_part = (
        real_part * twist_real - imag_part * twist_imag,
        real_part * twist_imag + imag_part * twist_real,
    )
    real_part, imag_part = complex_step(
        real_part, imag_part, "cska,kb->csba", fourier_table(inner_size, 1.0)
    )
    row_real, row_imag = fourier_table(row_count, 1.0)
    result = contract("csba,sr->crba", real_part, row_real) - contract(
        "csba,sr->crba", imag_part, row_imag
    )
    return result.reshape(channels, row_count, column_count)


def row_matrix(length):
    current = np.eye(length)
    details = []
    for level_index in range(LEVELS):
        width_now = current.shape[0]
        half_size = width_now // 2
        lower = np.zeros((half_size, width_now))
        upper = np.zeros((half_size, width_now))
        for target in range(half_size):
            for tap_index in range(8):
                lower[target, (2 * target + tap_index) % width_now] += low_pass[tap_index]
                upper[target, (2 * target + tap_index) % width_now] += high_pass[tap_index]
        details.insert(0, upper @ current)
        current = lower @ current
    return jnp.asarray(np.concatenate([current] + details, 0), jnp.float32)


def analysis_step(length):
    half_size = length // 2
    matrix = np.zeros((length + 6, length))
    for target in range(half_size):
        for tap_index in range(8):
            matrix[2 * target + tap_index, target] += low_pass[tap_index]
            matrix[2 * target + tap_index, half_size + target] += high_pass[tap_index]
    return jnp.asarray(matrix, jnp.float32)


def synthesis_step(length):
    matrix = np.zeros((2 * (length + 3), 2 * length))
    for source in range(length):
        for parity in range(2):
            for back_step in range(4):
                matrix[source - back_step + 3, 2 * source + parity] += low_pass[
                    parity + 2 * back_step
                ]
                matrix[length + 3 + source - back_step + 3, 2 * source + parity] += high_pass[
                    parity + 2 * back_step
                ]
    return jnp.asarray(matrix, jnp.float32)


def column_analysis(values, right_rim):
    coarse = values
    details = []
    for level_index in range(LEVELS):
        length = coarse.shape[-1]
        extended = jnp.concatenate([coarse, right_rim(coarse[..., :6])], -1)
        halves = contract("...m,mk->...k", extended, analysis_step(length))
        details.insert(0, halves[..., length // 2 :])
        coarse = halves[..., : length // 2]
    return jnp.concatenate([coarse] + details, -1)


def column_synthesis(coefficients, left_rim):
    length = coefficients.shape[-1] >> LEVELS
    coarse = coefficients[..., :length]
    offset = length
    for level_index in range(LEVELS):
        detail = coefficients[..., offset : offset + length]
        coarse_edge, detail_edge = left_rim(coarse[..., -3:], detail[..., -3:])
        extended = jnp.concatenate([coarse_edge, coarse, detail_edge, detail], -1)
        coarse = contract("...m,mk->...k", extended, synthesis_step(length))
        offset = offset + length
        length = length * 2
    return coarse


def right_within(edge_cols):
    return jnp.roll(edge_cols, -1, axis=-2)


def left_within(coarse_edge, detail_edge):
    return (jnp.roll(coarse_edge, 1, axis=-2), jnp.roll(detail_edge, 1, axis=-2))


def shards(sky_image, measured_real, measured_imaginary, sampling_mask, dual_field):
    channels, row_count, column_count = sky_image.shape
    rows_table = row_matrix(row_count)
    gradient = data_gradient(sky_image, measured_real, measured_imaginary, sampling_mask)
    facet_count = lax.axis_size("fac")
    facet_width = column_count // facet_count
    local_dual = lax.all_to_all(dual_field, "fac", split_axis=0, concat_axis=2, tiled=True)
    coefficients = local_dual.reshape(channels, row_count, facet_count, facet_width)
    prior_term = column_synthesis(coefficients, left_within).reshape(
        channels, row_count, column_count
    )
    prior_term = contract("sr,csn->crn", rows_table, prior_term)
    next_image = jnp.maximum(sky_image - primal_step * (gradient + prior_term), 0.0)
    analysed = contract("rs,csn->crn", rows_table, 2.0 * next_image - sky_image)
    analysed = column_analysis(
        analysed.reshape(channels, row_count, facet_count, facet_width), right_within
    )
    lifted = local_dual + dual_step * analysed.reshape(channels, row_count, column_count)
    summed = lax.psum(jnp.sum(lifted * lifted, axis=0), "fac")
    shrunk = lifted / jnp.maximum(1.0, jnp.sqrt(summed) / ball_radius)
    next_dual = lax.all_to_all(shrunk, "fac", split_axis=2, concat_axis=0, tiled=True)
    return (next_image, next_dual)


def solution(mesh):
    return jax.shard_map(
        shards,
        mesh=mesh,
        in_specs=(
            P(("groups", "fac"), None, None),
            P(("groups", "fac"), None, None),
            P(("groups", "fac"), None, None),
            P(("groups", "fac"), None, None),
            P("groups", None, "fac"),
        ),
        out_specs=(P(("groups", "fac"), None, None), P("groups", None, "fac")),
        check_vma=False,
    )
```

profile of v0, /device:TPU:0, one launch (start us, length us, event | category | flops | bytes accessed | tf_op | source)
XLA Modules:
  0.0 563.5 jit_solution(9362236796377634353)
XLA Ops:
  7.2 7.4 %all-to-all-start = ((f32[64,96,128]{2,1,0:T(8,128)}), f32[64,96,128]{2,1,0:T(8,128)}, u32[]{:S(2)}, u32[]{:S(2)}) async-start(f32[64,96,128]{2,1,0:T(8,128)} %param.34), calls=%async_computation | async-start | bytes 6291456 | tf_op jit(solution)/shard_map/all_to_all | solution.py:190
  14.7 3.3 copy.124
  18.0 5.8 %fusion.127 = f32[96,8192]{0,1:S(1)} fusion(f32[96,96]{1,0:T(8,128)S(1)} %copy-done.20, f32[96,8192]{0,1:T(8,128)} %bitcast.150), kind=kOutput, calls=%fused_computation.137 | convolution fusion | flops 905969664 | bytes 6328320
  23.8 3.6 fusion.126
  27.4 6.6 %fusion.37 = f32[2,96,64,64]{1,3,2,0:T(8,128)S(1)} fusion(f32[64,64,1,1]{0,1,3,2:T(8,128)S(1)} %copy-done.13, f32[2,96,64,64]{1,3,2,0:T(8,128)S(1)} %bitcast.154), kind=kOutput, calls=%fused_computation.56 | convolution fusion | flops 603979776 | bytes 6307840 | tf_op jit(solution)/shard_map/csba,bk->cska/dot_general | solution.py:28
  34.0 6.8 %fusion.35 = f32[2,96,64,64]{1,3,2,0:T(8,128)S(1)} fusion(f32[64,64,1,1]{0,1,3,2:T(8,128)S(1)} %copy-done.10, f32[2,96,64,64]{1,3,2,0:T(8,128)S(1)} %bitcast.155), kind=kOutput, calls=%fused_computation.54 | convolution fusion | flops 603979776 | bytes 6307840 | tf_op jit(solution)/shard_map/csba,bk->cska/dot_general | solution.py:28
  40.8 6.6 %fusion.60 = f32[2,96,64,64]{1,3,2,0:T(8,128)S(1)} fusion(f32[2,96,64,64]{1,3,2,0:T(8,128)S(1)} %fusion.37, f32[64,64,1,1]{0,1,3,2:T(8,128)S(1)} %copy-done.10, f32[2,96,64,64]{1,3,2,0:T(8,128)S(1)} %bitcast.152), kind=kOutput, calls=%fused_computation.80 | convolution fusion | flops 604766208 | bytes 9453568 | tf_op jit(solution)/shard_map/csba,bk->cska/dot_general | solution.py:28
  47.5 11.3 %fusion.13 = (f32[2,96,64,64]{1,2,3,0:T(8,128)}, f32[2,96,64,64]{1,2,3,0:T(8,128)S(1)}) fusion(f32[2,96,64,64]{1,3,2,0:T(8,128)S(1)} %fusion.60, f32[64,64]{0,1:T(8,128)S(1)} %copy-done.15, f32[64,64]{0,1:T(8,128)S(1)} %copy-done.9, f32[2,96,64,64]{1,3,2,0:T(8,128)S(1)} %fusion.35, f32[64,64,1,1]{0,1,3,2:T(8,128)S(1)} %copy-done.13, ...), kind=kOutput, calls=%fused_computation.20 | convolution fusion | flops 609484800 | bytes 15777792 | tf_op jit(solution)/shard_map/csba,bk->cska/dot_general | solution.py:28
  58.7 7.1 %fusion.29 = f32[2,96,64,64]{1,3,2,0:T(8,128)} fusion(f32[64,64,1,1]{0,1,3,2:T(8,128)S(1)} %copy-done.13, f32[2,96,64,64]{1,2,3,0:T(8,128)S(1)} %get-tuple-element.5), kind=kOutput, calls=%fused_computation.48 | convolution fusion | flops 603979776 | bytes 6307840 | tf_op jit(solution)/shard_map/cska,aj->csjk/dot_general | solution.py:28
  65.8 7.1 %fusion.27 = f32[2,96,64,64]{1,3,2,0:T(8,128)} fusion(f32[64,64,1,1]{0,1,3,2:T(8,128)S(1)} %copy-done.10, f32[2,96,64,64]{1,2,3,0:T(8,128)S(1)} %get-tuple-element.5), kind=kOutput, calls=%fused_computation.46 | convolution fusion | flops 603979776 | bytes 6307840 | tf_op jit(solution)/shard_map/cska,aj->csjk/dot_general | solution.py:28
  72.9 5.3 copy.132
  78.2 9.7 %subtract_bitcast_fusion.1 = f32[2,96,64,64]{1,2,3,0:T(8,128)S(1)} fusion(f32[2,96,64,64]{1,3,2,0:T(8,128)} %fusion.29, f32[64,64,1,1]{0,1,3,2:T(8,128)S(1)} %copy-done.10, f32[2,96,64,64]{1,2,3,0:T(8,128)} %get-tuple-element.4), kind=kOutput, calls=%fused_computation.37 | convolution fusion | flops 604766208 | bytes 9453568 | tf_op jit(solution)/shard_map/cska,aj->csjk/dot_general | solution.py:28
  87.8 4.4 copy.131
  92.2 5.1 copy.123
  97.4 5.3 copy.137
  102.7 9.7 %add_bitcast_fusion.1 = f32[2,96,64,64]{1,2,3,0:T(8,128)S(1)} fusion(f32[2,96,64,64]{1,3,2,0:T(8,128)} %fusion.27, f32[64,64,1,1]{0,1,3,2:T(8,128)S(1)} %copy-done.13, f32[2,96,64,64]{1,2,3,0:T(8,128)} %get-tuple-element.4), kind=kOutput, calls=%fused_computation.36 | convolution fusion | flops 604766208 | bytes 9453568 | tf_op jit(solution)/shard_map/cska,aj->csjk/dot_general | solution.py:28
  112.4 4.4 copy.136
  116.7 11.3 %fusion.12 = (f32[2,96,4096]{1,2,0:T(8,128)}, f32[2,96,4096]{1,2,0:T(8,128)}) fusion(f32[2,96,4096]{1,2,0:T(8,128)} %copy.132, f32[2,96,64,64]{1,3,2,0:T(8,128)} %copy.131, s32[2,96,4096]{1,2,0:T(8,128)} %copy.123, f32[2,96,4096]{1,2,0:T(8,128)} %copy.137, f32[2,96,64,64]{1,3,2,0:T(8,128)} %copy.136), kind=kLoop, calls=%fused_computation.17 | loop fusion | flops 3932160 | bytes 22020096 | tf_op jit(solution)/shard_map/mul | solution.py:85
  128.0 10.9 %fusion.19 = f32[2,96,64,64]{1,3,2,0:T(8,128)} fusion(f32[64,64,1,1]{0,1,3,2:T(8,128)S(1)} %copy-done.10, f32[2,96,64,64]{1,3,2,0:T(8,128)} %bitcast.164), kind=kOutput, calls=%fused_computation.38 | convolution fusion | flops 603979776 | bytes 6307840 | tf_op jit(solution)/shard_map/csjk,ja->cska/dot_general | solution.py:28
  138.9 7.1 %fusion.21 = f32[2,96,64,64]{1,3,2,0:T(8,128)} fusion(f32[64,64,1,1]{0,1,3,2:T(8,128)S(1)} %copy-done.12, f32[2,96,64,64]{1,3,2,0:T(8,128)S(1)} %bitcast.165), kind=kOutput, calls=%fused_computation.40 | convolution fusion | flops 603979776 | bytes 6307840 | tf_op jit(solution)/shard_map/csjk,ja->cska/dot_general | solution.py:28
  146.0 7.1 %fusion.23 = f32[2,96,64,64]{1,3,2,0:T(8,128)} fusion(f32[64,64,1,1]{0,1,3,2:T(8,128)S(1)} %copy-done.12, f32[2,96,64,64]{1,3,2,0:T(8,128)S(1)} %bitcast.162), kind=kOutput, calls=%fused_computation.42 | convolution fusion | flops 603979776 | bytes 6307840 | tf_op jit(solution)/shard_map/csjk,ja->cska/dot_general | solution.py:28
  153.1 7.2 %fusion.25 = f32[2,96,64,64]{1,3,2,0:T(8,128)} fusion(f32[64,64,1,1]{0,1,3,2:T(8,128)S(1)} %copy-done.10, f32[2,96,64,64]{1,3,2,0:T(8,128)S(1)} %bitcast.163), kind=kOutput, calls=%fused_computation.44 | convolution fusion | flops 603979776 | bytes 6307840 | tf_op jit(solution)/shard_map/csjk,ja->cska/dot_general | solution.py:28
  160.3 17.0 %copy_add_fusion = (f32[2,96,64,64]{1,2,3,0:T(8,128)S(1)}, f32[2,96,64,64]{1,2,3,0:T(8,128)}) fusion(f32[2,96,64,64]{1,3,2,0:T(8,128)} %fusion.19, f32[2,96,64,64]{1,3,2,0:T(8,128)} %fusion.23, f32[2,96,64,64]{1,3,2,0:T(8,128)} %fusion.21, f32[2,96,64,64]{1,3,2,0:T(8,128)} %fusion.25), kind=kLoop, calls=%fused_computation.29 | loop fusion | flops 1572864 | bytes 18874368 | tf_op jit(solution)/shard_map/add | solution.py:61
  177.3 6.7 %fusion.74 = f32[2,96,64,64]{1,3,2,0:T(8,128)S(1)} fusion(f32[64,64,1,1]{0,1,3,2:T(8,128)S(1)} %copy-done.12, f32[2,96,64,64]{1,2,3,0:T(8,128)S(1)} %get-tuple-element.26, f32[2,96,64,64]{1,2,3,0:T(8,128)} %get-tuple-element.27, f32[64,64]{0,1:T(8,128)S(1)} %copy-done.11, f32[64,64]{0,1:T(8,128)S(1)} %copy-done.9), kind=kOutput, calls=%fused_computation.85 | convolution fusion | flops 606339072 | bytes 9486336 | tf_op jit(solution)/shard_map/cska,kb->csba/dot_general | solution.py:28
  184.1 5.5 add_bitcast_fusion
  189.6 6.5 %fusion.15 = f32[2,64,64,96]{3,2,1,0:T(8,128)S(1)} fusion(f32[96,96,1,1]{1,0,3,2:T(8,128)S(1)} %copy-done.19, f32[2,96,64,64]{1,2,3,0:T(8,128)S(1)} %add_bitcast_fusion), kind=kOutput, calls=%fused_computation.25 | convolution fusion | flops 905969664 | bytes 6328320 | tf_op jit(solution)/shard_map/csba,sr->crba/dot_general | solution.py:28
  196.1 5.3 fusion.75
  201.5 5.3 subtract_bitcast_fusion
  206.8 7.4 %fusion.70 = f32[2,64,64,96]{3,2,1,0:T(8,128)} fusion(f32[2,64,64,96]{3,2,1,0:T(8,128)S(1)} %fusion.15, f32[96,96,1,1]{1,0,3,2:T(8,128)S(1)} %copy-done.18, f32[2,96,64,64]{1,2,3,0:T(8,128)S(1)} %subtract_bitcast_fusion), kind=kOutput, calls=%fused_computation.82 | convolution fusion | flops 906756096 | bytes 9474048 | tf_op jit(solution)/shard_map/csba,sr->crba/dot_general | solution.py:28
  214.2 5.3 copy.149
  219.5 5.2 copy.147
  224.7 1.9 slice.211
  230.3 2.5 fusion.48
  232.9 2.6 pad_maximum_fusion
  235.5 7.8 %copy.148 = f32[2,96,32,134]{3,2,1,0:T(8,128)} copy(f32[2,96,32,134]{1,3,2,0:T(8,128)} %pad_maximum_fusion) | data formatting | bytes 6586368 | tf_op jit(solution)/shard_map/concatenate | solution.py:169
  243.3 8.3 %fusion.128 = f32[2,96,32,128]{3,2,1,0:T(8,128)} fusion(f32[2,96,32,134]{3,2,1,0:T(8,128)} %copy.148, f32[134,128,1,1]{1,0,3,2:T(8,128)S(1)} %copy-done.17), kind=kOutput, calls=%fused_computation.138 | convolution fusion | flops 1264582656 | bytes 6507520 | tf_op jit(solution)/shard_map/...m,mk->...k/dot_general | solution.py:28
  251.6 4.9 reshape.48
  256.5 6.3 %fusion.9 = f32[2,96,4096]{2,1,0:T(8,128)S(1)} fusion(f32[2,96,4096]{2,1,0:T(8,128)S(1)} %copy-done.6, f32[2,96,4096]{2,1,0:T(8,128)} %copy.149, f32[2,96,4096]{2,1,0:T(8,128)} %reshape.48, f32[96,96,1]{0,1,2:T(8,128)S(1)} %copy-done.14), kind=kOutput, calls=%fused_computation.10 | convolution fusion | flops 909115392 | bytes 12619776 | tf_op jit(solution)/shard_map/sr,csn->crn/dot_general | solution.py:28
  262.9 3.3 fusion.45
  267.7 5.5 fusion
  276.0 8.4 %fusion.43 = f32[2,96,32,64]{1,3,2,0:T(8,128)S(1)} fusion(f32[70,64,1,1]{0,1,3,2:T(8,128)S(1)} %copy-done.22, f32[2,96,32,70]{3,2,1,0:T(8,128)S(1)} %maximum_maximum_fusion), kind=kOutput, calls=%fused_computation.63 | convolution fusion | flops 330301440 | bytes 3311104 | tf_op jit(solution)/shard_map/...m,mk->...k/dot_general | solution.py:28
  287.9 3.1 copy.170
  292.7 7.0 %multiply_reduce_fusion = (f32[96,32,128]{0,2,1:T(8,128)}, f32[2,96,32,128]{1,3,2,0:T(8,128)}) fusion(f32[2,96,32,64]{1,3,2,0:T(8,128)} %copy.170, f32[2,96,32,32]{1,3,2,0:T(8,128)} %get-tuple-element.23, f32[2,96,32,16]{1,3,2,0:T(8,128)} %get-tuple-element.25, f32[2,96,32,16]{1,3,2,0:T(8,128)S(1)} %fusion.106, f32[32,2,96,128]{2,3,0,1:T(8,128)} %copy.147), kind=kLoop, calls=%fused_computation.31 | loop fusion | flops 5111808 | bytes 11010048 | tf_op jit(solution)/shard_map/reduce_sum | solution.py:202
  299.6 135.1 %all-reduce.2.cloned.1.call-done = f32[96,4096]{0,1:T(8,128)} async-done(((f32[96,4096]{0,1:T(8,128)}), f32[96,4096]{0,1:T(8,128)}) %all-reduce.2.cloned.1.call-update) | async-done | bytes 1572880 | tf_op jit(solution)/shard_map/psum | solution.py:202
  434.7 2.4 multiply_maximum_fusion
  437.6 15.1 %copy_divide_fusion = f32[2,96,4096]{1,0,2:T(2,128)S(1)} fusion(f32[2,96,4096]{1,2,0:T(8,128)S(1)} %bitcast.169, f32[96,4096]{0,1:T(8,128)S(1)} %multiply_maximum_fusion), kind=kLoop, calls=%fused_computation.24 | loop fusion | flops 786432 | bytes 7864320 | tf_op jit(solution)/shard_map/div | solution.py:203
  452.7 97.1 %all_to_all.33 = f32[2,96,4096]{1,0,2:T(2,128)} all-to-all(f32[2,96,4096]{1,0,2:T(2,128)S(1)} %copy_divide_fusion), channel_id=1, replica_groups=mesh['groups'=1,'fac'=32] {'fac'}, dimensions={2} | all-to-all | bytes 6291456 | tf_op jit(solution)/shard_map/all_to_all | solution.py:204
  549.8 6.6 %copy.154 = f32[32,2,96,128]{3,2,1,0:T(8,128)} copy(f32[32,2,96,128]{2,1,3,0:T(2,128)} %bitcast.171) | data formatting | bytes 6291456 | tf_op jit(solution)/shard_map/all_to_all | solution.py:204
  (87 shorter events, 13.6 us)
Async XLA Ops:
  7.2 7.5 %copy-start.5 = (f32[2,96,4096]{2,1,0:T(8,128)S(1)}, f32[2,96,4096]{2,1,0:T(8,128)}, u32[]{:S(2)}) copy-start(f32[2,96,4096]{2,1,0:T(8,128)} %param.30) | copy-start | bytes 9437188
  7.2 212.3 %all-to-all-start = ((f32[64,96,128]{2,1,0:T(8,128)}), f32[64,96,128]{2,1,0:T(8,128)}, u32[]{:S(2)}, u32[]{:S(2)}) async-start(f32[64,96,128]{2,1,0:T(8,128)} %param.34), calls=%async_computation | async-start | bytes 6291456 | tf_op jit(solution)/shard_map/all_to_all | solution.py:190
  14.6 3.4 copy-start.20
  14.6 420.1 %all-reduce.2.cloned.1.call-start = ((), (), s32[]{:S(2)}) async-start(), calls=%async_computation.2 | async-start | bytes 4194304 | tf_op jit(solution)/shard_map/psum | solution.py:202
  18.0 5.8 %copy-start.1 = (f32[2,96,4096]{1,2,0:T(8,128)S(1)}, f32[2,96,4096]{1,2,0:T(8,128)}, u32[]{:S(2)}) copy-start(f32[2,96,4096]{1,2,0:T(8,128)} %copy.124) | copy-start | bytes 9437188
  18.0 5.8 %copy-start.21 = (f32[96,96]{1,0:T(8,128)S(1)}, f32[96,96]{1,0:T(8,128)}, u32[]{:S(2)}) copy-start(f32[96,96]{1,0:T(8,128)} %constant.51.clone) | copy-start | bytes 110596
  23.8 3.6 copy-start.13
  27.4 6.6 %copy-start.10 = (f32[64,64,1,1]{0,1,3,2:T(8,128)S(1)}, f32[64,64,1,1]{0,1,3,2:T(8,128)}, u32[]{:S(2)}) copy-start(f32[64,64,1,1]{0,1,3,2:T(8,128)} %constant.72) | copy-start | bytes 49156
  40.8 6.6 %copy-start.9 = (f32[64,64]{0,1:T(8,128)S(1)}, f32[64,64]{0,1:T(8,128)}, u32[]{:S(2)}) copy-start(f32[64,64]{0,1:T(8,128)} %constant.55.clone) | copy-start | bytes 49156
  40.8 6.6 %copy-start.15 = (f32[64,64]{0,1:T(8,128)S(1)}, f32[64,64]{0,1:T(8,128)}, u32[]{:S(2)}) copy-start(f32[64,64]{0,1:T(8,128)} %constant.56.clone) | copy-start | bytes 49156
  128.0 10.9 %copy-start.4 = (f32[2,96,4096]{1,2,0:T(8,128)S(1)}, f32[2,96,4096]{1,2,0:T(8,128)}, u32[]{:S(2)}) copy-start(f32[2,96,4096]{1,2,0:T(8,128)} %get-tuple-element.19) | copy-start | bytes 9437188
  128.0 10.9 %copy-start.12 = (f32[64,64,1,1]{0,1,3,2:T(8,128)S(1)}, f32[64,64,1,1]{0,1,3,2:T(8,128)}, u32[]{:S(2)}) copy-start(f32[64,64,1,1]{0,1,3,2:T(8,128)} %constant.74) | copy-start | bytes 49156
  138.9 7.1 %copy-start.3 = (f32[2,96,4096]{1,2,0:T(8,128)S(1)}, f32[2,96,4096]{1,2,0:T(8,128)}, u32[]{:S(2)}) copy-start(f32[2,96,4096]{1,2,0:T(8,128)} %get-tuple-element.18) | copy-start | bytes 9437188
  160.3 17.0 %copy-start.11 = (f32[64,64]{0,1:T(8,128)S(1)}, f32[64,64]{0,1:T(8,128)}, u32[]{:S(2)}) copy-start(f32[64,64]{0,1:T(8,128)} %constant.58.clone) | copy-start | bytes 49156
  177.3 6.7 %copy-start = (f32[2,96,64,64]{1,2,3,0:T(8,128)S(1)}, f32[2,96,64,64]{1,2,3,0:T(8,128)}, u32[]{:S(2)}) copy-start(f32[2,96,64,64]{1,2,3,0:T(8,128)} %get-tuple-element.27) | copy-start | bytes 9437188
  184.0 5.6 copy-start.19
  201.5 5.4 copy-start.18
  224.7 2.8 copy-start.2
  224.7 3.2 copy-start.27
  227.5 1.3 copy-start.26
  227.8 2.6 copy-start.25
  235.5 7.8 %copy-start.17 = (f32[134,128,1,1]{1,0,3,2:T(8,128)S(1)}, f32[134,128,1,1]{1,0,3,2:T(8,128)}, u32[]{:S(2)}) copy-start(f32[134,128,1,1]{1,0,3,2:T(8,128)} %constant.80) | copy-start | bytes 205828
  251.6 4.9 copy-start.6
  251.6 5.0 copy-start.14
  262.8 3.4 copy-start.8
  266.8 0.9 copy-start.16
  274.8 1.1 copy-start.22
  276.0 9.6 %copy-start.23 = (f32[38,32,1,1]{0,1,3,2:T(8,128)S(1)}, f32[38,32,1,1]{0,1,3,2:T(8,128)}, u32[]{:S(2)}) copy-start(f32[38,32,1,1]{0,1,3,2:T(8,128)} %constant.84) | copy-start | bytes 14596
  286.7 4.2 copy-start.24
  434.7 2.8 copy-start.7
Sparse Core Ops, SparseCore 0:
  299.8 134.9 all-reduce.1
where the time goes:
time: 567 us; the launch traced here: 563 us
  matrix products  183 us (32%)
  waiting for transfers between devices  135 us (24%)
  blocking collectives  97.1 us (17%)
  local copies, waits for them, and re-layouts  69.9 us (12%)
  other arithmetic  56.4 us (10%)
  between operations  14.9 us (3%)
  starting transfers between devices  7.46 us (1%)
    dot_general x28, matrix products, contract(): jnp.einsum(pattern, left_side, right_side, precision=precise, preferred_e...  173 us
    psum x1, waiting for transfers between devices, shards(): summed = lax.psum(jnp.sum(lifted * lifted, axis=0), 'fac')  135 us
    all_to_all x1, blocking collectives, shards(): lax.all_to_all(shrunk, 'fac', split_axis=2, concat_axis=0, tiled=True)  97.1 us
    unnamed x62, local copies, waits for them, and re-layouts  24.6 us
    add x1, other arithmetic, complex_step(): contract(pattern, real_part, matrix[1])  17 us
    div x1, other arithmetic, shards(): shrunk = lifted / jnp.maximum(1.0, jnp.sqrt(summed) / ball_radius)  15.1 us
  transfers between devices with their start and end apart: 2, of which 1 were waited for; matrix products, arithmetic and copies ran while one was open for 36% of the time, Pallas kernels for 0%

commit v1 on v0

v1 whole, which is shorter than its diff:
```python
import functools

import jax
import jax.numpy as jnp
import numpy as np
from jax import lax
from jax.experimental import pallas as pl
from jax.experimental.pallas import tpu as pltpu
from jax.sharding import PartitionSpec as P

LEVELS = 4
LANES = 128

low_pass = (
    0.2303778133088964,
    0.7148465705529155,
    0.6308807679298587,
    -0.0279837694168599,
    -0.1870348117190931,
    0.0308413818355607,
    0.0328830116668852,
    -0.010597401785069,
)
high_pass = tuple(((-1) ** tap_index * low_pass[7 - tap_index] for tap_index in range(8)))
primal_step = 0.6
dual_step = 0.8
ball_radius = 12.0
f32 = jnp.float32
bf16 = jnp.bfloat16


def halves(matrix):
    high = np.asarray(matrix, np.float32).astype(bf16)
    low = (np.asarray(matrix, np.float64) - high.astype(np.float64)).astype(bf16)
    return high, low


def split(values):
    high = values.astype(bf16)
    low = (values - high.astype(f32)).astype(bf16)
    return high, low


def mul(left, right):
    return jnp.dot(left, right, preferred_element_type=f32)


def row_fourier(rows):
    grid = np.arange(rows)
    angles = 2.0 * np.pi * (np.outer(grid, grid) % rows) / rows
    return np.concatenate([np.cos(angles), -np.sin(angles)], 0) / np.sqrt(rows)


def lane_fourier(scale):
    grid = np.arange(LANES)
    angles = 2.0 * np.pi * (np.outer(grid, grid) % LANES) / LANES
    cosine, sine = np.cos(angles), np.sin(angles)
    return np.block([[cosine, -sine], [sine, cosine]]) * scale


def twiddles(slabs, columns):
    angles = 2.0 * np.pi * np.outer(np.arange(slabs), np.arange(LANES)) / columns
    table = np.stack([np.cos(angles), -np.sin(angles)], 1)
    return np.broadcast_to(table[:, :, None, :], (slabs, 2, 8, LANES)).astype(np.float32)


def row_wavelet(length):
    current = np.eye(length)
    details = []
    for level_index in range(LEVELS):
        width_now = current.shape[0]
        half_size = width_now // 2
        lower = np.zeros((half_size, width_now))
        upper = np.zeros((half_size, width_now))
        for target in range(half_size):
            for tap_index in range(8):
                lower[target, (2 * target + tap_index) % width_now] += low_pass[tap_index]
                upper[target, (2 * target + tap_index) % width_now] += high_pass[tap_index]
        details.insert(0, upper @ current)
        current = lower @ current
    return np.concatenate([current] + details, 0)


def facet_wavelet(width):
    needed = [width >> LEVELS]
    for level_index in range(LEVELS):
        needed.insert(0, 2 * (needed[0] - 1) + 8)
    current = np.eye(2 * width)
    details = []
    for level_index in range(LEVELS):
        count = needed[level_index + 1]
        lower = np.zeros((count, 2 * width))
        upper = np.zeros((count, 2 * width))
        for target in range(count):
            for tap_index in range(8):
                lower[target] += low_pass[tap_index] * current[2 * target + tap_index]
                upper[target] += high_pass[tap_index] * current[2 * target + tap_index]
        details.insert(0, upper[: width >> (level_index + 1)])
        current = lower
    matrix = np.concatenate([current[: width >> LEVELS]] + details, 0).T
    return np.concatenate([matrix[:width], matrix[width:]], 1)


def turn(value, step, length, sign):
    real, imag = value
    step = step % length
    if step == 0:
        return real, imag
    if 4 * step == length:
        return (-imag, real) if sign > 0 else (imag, -real)
    if 8 * step == length:
        root = float(np.sqrt(0.5))
        if sign > 0:
            return (real - imag) * root, (real + imag) * root
        return (real + imag) * root, (imag - real) * root
    if 8 * step == 3 * length:
        root = float(np.sqrt(0.5))
        if sign > 0:
            return (real + imag) * (-root), (real - imag) * root
        return (imag - real) * root, (real + imag) * (-root)
    cosine = float(np.cos(2.0 * np.pi * step / length))
    sine = float(sign * np.sin(2.0 * np.pi * step / length))
    return real * cosine - imag * sine, real * sine + imag * cosine


def short_transform(values, sign):
    length = len(values)
    if length == 1:
        return values
    even = short_transform(values[0::2], sign)
    odd = short_transform(values[1::2], sign)
    first, second = [], []
    for step in range(length // 2):
        real, imag = turn(odd[step], step, length, sign)
        first.append((even[step][0] + real, even[step][1] + imag))
        second.append((even[step][0] - real, even[step][1] - imag))
    return first + second


def fidelity_kernel(
    sky, real, imag, mask, row_hi, row_lo, back_hi, back_lo, lane_hi, lane_lo,
    inv_hi, inv_lo, twist, base, row_part, slab_part,
):
    rows, columns = sky.shape[1], sky.shape[2]
    slabs = columns // LANES
    width = 512

    def rows_forward(index, carry):
        lanes = pl.ds(pl.multiple_of(index * width, width), width)
        high, low = split(sky[0, :, lanes])
        row_part[:, lanes] = mul(row_hi[...], high) + mul(row_hi[...], low) + mul(row_lo[...], high)
        return carry

    lax.fori_loop(0, columns // width, rows_forward, 0)

    def slabs_forward(index, carry):
        start = pl.multiple_of(index * 8, 8)
        values = []
        for slab in range(slabs):
            lanes = slice(slab * LANES, (slab + 1) * LANES)
            values.append(
                (row_part[pl.ds(start, 8), lanes], row_part[pl.ds(start + rows, 8), lanes])
            )
        for slab, (re, im) in enumerate(short_transform(values, -1)):
            if slab:
                tr, ti = twist[slab, 0], twist[slab, 1]
                re, im = re * tr - im * ti, re * ti + im * tr
            slab_part[slab, pl.ds(start, 8), :LANES] = re
            slab_part[slab, pl.ds(start, 8), LANES:] = im
        return carry

    lax.fori_loop(0, rows // 8, slabs_forward, 0)

    def lanes_both(slab, carry):
        high, low = split(slab_part[slab])
        found = mul(high, lane_hi[...]) + mul(low, lane_hi[...]) + mul(high, lane_lo[...])
        weight = mask[0, slab].astype(f32)
        re = weight * (found[:, :LANES] - real[0, slab])
        im = weight * (found[:, LANES:] - imag[0, slab])
        high, low = split(jnp.concatenate([re, im], 1))
        slab_part[slab] = mul(high, inv_hi[...]) + mul(low, inv_hi[...]) + mul(high, inv_lo[...])
        return carry

    lax.fori_loop(0, slabs, lanes_both, 0)

    def slabs_back(index, carry):
        start = pl.multiple_of(index * 8, 8)
        values = []
        for slab in range(slabs):
            re = slab_part[slab, pl.ds(start, 8), :LANES]
            im = slab_part[slab, pl.ds(start, 8), LANES:]
            if slab:
                tr, ti = twist[slab, 0], twist[slab, 1]
                re, im = re * tr + im * ti, im * tr - re * ti
            values.append((re, im))
        for slab, (re, im) in enumerate(short_transform(values, 1)):
            lanes = slice(slab * LANES, (slab + 1) * LANES)
            row_part[pl.ds(start, 8), lanes] = re
            row_part[pl.ds(start + rows, 8), lanes] = im
        return carry

    lax.fori_loop(0, rows // 8, slabs_back, 0)

    def rows_back(index, carry):
        lanes = pl.ds(pl.multiple_of(index * width, width), width)
        high, low = split(row_part[:, lanes])
        gradient = mul(back_hi[...], high) + mul(back_hi[...], low) + mul(back_lo[...], high)
        base[0, :, lanes] = sky[0, :, lanes] - primal_step * gradient
        return carry

    lax.fori_loop(0, columns // width, rows_back, 0)


def whole(array):
    return pl.BlockSpec(array.shape, lambda *index: (0,) * array.ndim)


def fidelity(sky, real, imag, mask):
    channels, rows, columns = sky.shape
    slabs = columns // LANES

    def by_slab(values):
        return values.reshape(channels, rows, LANES, slabs).transpose(0, 3, 1, 2)

    forward = row_fourier(rows)
    lane = lane_fourier(1.0 / np.sqrt(columns))
    tables = (
        *halves(forward), *halves(forward.T), *halves(lane), *halves(lane.T),
        twiddles(slabs, columns),
    )
    tables = tuple(jnp.asarray(table) for table in tables)
    image = pl.BlockSpec((1, rows, columns), lambda c: (c, 0, 0))
    slab = pl.BlockSpec((1, slabs, rows, LANES), lambda c: (c, 0, 0, 0))
    return pl.pallas_call(
        fidelity_kernel,
        out_shape=jax.ShapeDtypeStruct(sky.shape, f32),
        grid=(channels,),
        in_specs=[image, slab, slab, slab, *(whole(table) for table in tables)],
        out_specs=image,
        scratch_shapes=[
            pltpu.VMEM((2 * rows, columns), f32),
            pltpu.VMEM((slabs, rows, 2 * LANES), f32),
        ],
        compiler_params=pltpu.CompilerParams(vmem_limit_bytes=56 << 20),
        name="fidelity",
    )(sky, by_slab(real), by_slab(imag), by_slab(mask), *tables)


def prior_kernel(
    coef, base, sky, synth2, synth_lo, rowt2, rowt_lo, row2, row_lo, ana2, ana_lo,
    image, out, part_hi, part_lo, after,
):
    facets, rows, width = coef.shape[0], coef.shape[2], coef.shape[3]

    def spread(facet):
        high, low = split(coef[facet, 0])
        return mul(jnp.concatenate([high, low], 1), synth2[...]) + mul(high, synth_lo[...])

    before = spread(facets - 1)[:, width:]
    for facet in range(facets):
        both = spread(facet)
        high, low = split(both[:, :width] + before)
        before = both[:, width:]
        lanes = slice(facet * width, (facet + 1) * width)
        part_hi[:, lanes] = high
        part_lo[:, lanes] = low

    wide = 2 * width
    for index in range(facets // 2):
        lanes = slice(index * wide, (index + 1) * wide)
        high, low = part_hi[:, lanes], part_lo[:, lanes]
        step = mul(rowt2[...], jnp.concatenate([high, low], 0)) + mul(rowt_lo[...], high)
        fresh = jnp.maximum(base[0, :, lanes] - step, 0.0)
        image[0, :, lanes] = fresh
        high, low = split(2.0 * fresh - sky[0, :, lanes])
        turned = mul(row2[...], jnp.concatenate([high, low], 0)) + mul(row_lo[...], high)
        high, low = split(turned)
        for half in range(2):
            facet = 2 * index + half
            mine = slice(half * width, (half + 1) * width)
            both = mul(
                jnp.concatenate([high[:, mine], low[:, mine]], 1), ana2[...]
            ) + mul(high[:, mine], ana_lo[...])
            if facet:
                out[facet - 1, 0] = after[...] + both[:, width:]
                after[...] = both[:, :width]
            else:
                out[facets - 1, 0] = both[:, width:]
                after[...] = both[:, :width]
    out[facets - 1, 0] = after[...] + out[facets - 1, 0]


def prior(coefs, base, sky):
    channels, rows, columns = sky.shape
    facets, width = coefs.shape[0], coefs.shape[3]
    facet_table = facet_wavelet(width)
    own, other = facet_table[:, :width], facet_table[:, width:]
    synth = halves(np.concatenate([own.T, other.T], 1))
    analysis = halves(dual_step * facet_table)
    row_table = row_wavelet(rows)
    rowt = halves(primal_step * row_table.T)
    row = halves(row_table)
    tables = (
        np.concatenate([synth[0], synth[0]], 0), synth[1],
        np.concatenate([rowt[0], rowt[0]], 1), rowt[1],
        np.concatenate([row[0], row[0]], 1), row[1],
        np.concatenate([analysis[0], analysis[0]], 0), analysis[1],
    )
    tables = tuple(jnp.asarray(table) for table in tables)
    image = pl.BlockSpec((1, rows, columns), lambda c: (c, 0, 0))
    facet = pl.BlockSpec((facets, 1, rows, width), lambda c: (0, c, 0, 0))
    return pl.pallas_call(
        prior_kernel,
        out_shape=(
            jax.ShapeDtypeStruct(sky.shape, f32),
            jax.ShapeDtypeStruct(coefs.shape, f32),
        ),
        grid=(channels,),
        in_specs=[facet, image, image, *(whole(table) for table in tables)],
        out_specs=(image, facet),
        scratch_shapes=[
            pltpu.VMEM((rows, columns), bf16),
            pltpu.VMEM((rows, columns), bf16),
            pltpu.VMEM((rows, width), f32),
        ],
        compiler_params=pltpu.CompilerParams(vmem_limit_bytes=56 << 20),
        name="prior",
    )(coefs, base, sky, *tables)


def shrink_kernel(dual, change, out):
    lifted = dual[...] + change[...]
    norm = jnp.sqrt(jnp.sum(lifted * lifted, 0))
    out[...] = lifted * (1.0 / jnp.maximum(1.0, norm / ball_radius))[None]


def shrink(dual, change):
    channels, rows, width = dual.shape
    step = 8
    block = pl.BlockSpec((channels, step, width), lambda r: (0, r, 0))
    return pl.pallas_call(
        shrink_kernel,
        out_shape=jax.ShapeDtypeStruct(dual.shape, f32),
        grid=(rows // step,),
        in_specs=[block, block],
        out_specs=block,
        compiler_params=pltpu.CompilerParams(vmem_limit_bytes=56 << 20),
        name="shrink",
    )(dual, change)


def shards(sky_image, measured_real, measured_imaginary, sampling_mask, dual_field):
    channels, row_count, column_count = sky_image.shape
    facets = lax.axis_size("fac")
    width = column_count // facets
    sent = dual_field.reshape(facets, channels, row_count, width)
    coefs = lax.all_to_all(sent, "fac", split_axis=0, concat_axis=0, tiled=True)
    base = fidelity(sky_image, measured_real, measured_imaginary, sampling_mask)
    next_image, change = prior(coefs, base, sky_image)
    change = lax.all_to_all(change, "fac", split_axis=0, concat_axis=0, tiled=True)
    next_dual = shrink(dual_field, change.reshape(dual_field.shape))
    return (next_image, next_dual)


def solution(mesh):
    split_channels = P(("groups", "fac"), None, None)
    split_facets = P("groups", None, "fac")
    return jax.shard_map(
        shards,
        mesh=mesh,
        in_specs=(split_channels,) * 4 + (split_facets,),
        out_specs=(split_channels, split_facets),
        check_vma=False,
    )
```

time: 567 us -> 193 us (0.34)
  matrix products: 183 us -> 0 us
  waiting for transfers between devices: 135 us -> 0.01 us
  Pallas kernels: 0 us -> 74.9 us
  other arithmetic: 56.4 us -> 0 us
  local copies, waits for them, and re-layouts: 69.9 us -> 32.5 us
  blocking collectives: 97.1 us -> 77.1 us
  between operations: 14.9 us -> 0.65 us
    dot_general x28 -> x0, matrix products: 173 us -> none  [contract(): jnp.einsum(pattern, left_side, right_side, precision=precise, preferred_e...]
    psum x1 -> x0, waiting for transfers between devices: 135 us -> none  [shards(): summed = lax.psum(jnp.sum(lifted * lifted, axis=0), 'fac')]
    pallas_call x0 -> x3, Pallas kernels: none -> 74.9 us  [the longest x1 47.5 us: fidelity(): pl.pallas_call(fidelity_kernel, out_shape=jax.ShapeDtypeStruct(sky.shape,...]
    all_to_all x1, blocking collectives: 97.1 us -> 77.1 us  [shards(): lax.all_to_all(change, 'fac', split_axis=0, concat_axis=0, tiled=True)]
    add x1 -> x0, other arithmetic: 17 us -> none  [complex_step(): contract(pattern, real_part, matrix[1])]
    div x1 -> x0, other arithmetic: 15.1 us -> none  [shards(): shrunk = lifted / jnp.maximum(1.0, jnp.sqrt(summed) / ball_radius)]
    all_to_all x2 -> x0, local copies, waits for them, and re-layouts: 11.8 us -> none  [the longest x1 6.6 us: shards(): lax.all_to_all(shrunk, 'fac', split_axis=2, concat_axis=0, tiled=True)]
    mul x1 -> x0, other arithmetic: 11.3 us -> none  [data_gradient(): weights * (real_part.reshape(channels, row_count, column_count) - measure...]
  transfers between devices with their start and end apart: 2 -> 1, of which waited for: 1 -> 0; matrix products, arithmetic and copies ran while one was open for 36% -> 16% of each run, Pallas kernels for 0% -> 25%
where the time goes in v1:
time: 193 us; the launch traced here: 192 us
  blocking collectives  77.1 us (40%)
  Pallas kernels  74.9 us (39%)
  local copies, waits for them, and re-layouts  32.5 us (17%)
  starting transfers between devices  7.3 us (4%)
    all_to_all x1, blocking collectives, shards(): lax.all_to_all(change, 'fac', split_axis=0, concat_axis=0, tiled=True)  77.1 us
    pallas_call x1, Pallas kernels, fidelity(): pl.pallas_call(fidelity_kernel, out_shape=jax.ShapeDtypeStruct(sky.shape,...  47.5 us
    pallas_call x1, Pallas kernels, prior(): pl.pallas_call(prior_kernel, out_shape=(jax.ShapeDtypeStruct(sky.shape, f...  18.6 us
    unnamed x5, local copies, waits for them, and re-layouts  17 us
    reshape x3, local copies, waits for them, and re-layouts, by_slab(): return values.reshape(channels, rows, LANES, slabs).transpose(0, 3, 1, 2)  15.5 us
    pallas_call x1, Pallas kernels, shrink(): pl.pallas_call(shrink_kernel, out_shape=jax.ShapeDtypeStruct(dual.shape,...  8.9 us
    all_to_all x1, starting transfers between devices, shards(): coefs = lax.all_to_all(sent, 'fac', split_axis=0, concat_axis=0, tiled=True)  7.3 us
  transfers between devices with their start and end apart: 1, of which 0 were waited for; matrix products, arithmetic and copies ran while one was open for 16% of the time, Pallas kernels for 25%

profile of v1, /device:TPU:0, one launch (start us, length us, event | category | flops | bytes accessed | tf_op | source)
XLA Modules:
  0.0 192.5 jit_solution(6689126429314908989)
XLA Ops:
  0.6 7.3 %all-to-all-start = ((f32[32,2,96,128]{3,2,1,0:T(8,128)}), f32[32,2,96,128]{3,2,1,0:T(8,128)S(1)}, u32[]{:S(2)}, u32[]{:S(2)}) async-start(f32[32,2,96,128]{3,2,1,0:T(8,128)} %bitcast.11), calls=%async_computation | async-start | bytes 6291456 | tf_op jit(solution)/shard_map/all_to_all | solution.py:357
  7.9 5.1 %copy.24 = f32[2,96,4096]{1,2,0:T(8,128)} copy(f32[2,96,4096]{2,1,0:T(8,128)} %param.23) | data formatting | bytes 6291456 | tf_op args[1]
  13.1 5.1 %copy.25 = f32[2,96,128,32]{2,1,3,0:T(8,128)} copy(f32[2,96,128,32]{1,3,2,0:T(8,128)} %bitcast.8) | data formatting | bytes 6291456 | tf_op jit(solution)/shard_map/reshape | solution.py:223
  18.2 5.1 %copy.26 = f32[2,96,4096]{1,2,0:T(8,128)} copy(f32[2,96,4096]{2,1,0:T(8,128)} %param.24) | data formatting | bytes 6291456 | tf_op args[2]
  23.3 5.1 %copy.27 = f32[2,96,128,32]{2,1,3,0:T(8,128)} copy(f32[2,96,128,32]{1,3,2,0:T(8,128)} %bitcast.9) | data formatting | bytes 6291456 | tf_op jit(solution)/shard_map/reshape | solution.py:223
  28.5 5.1 %copy.28 = s32[2,96,4096]{1,2,0:T(8,128)} copy(s32[2,96,4096]{2,1,0:T(8,128)} %param.25) | data formatting | bytes 6291456 | tf_op args[3]
  33.6 5.2 %copy.29 = s32[2,96,128,32]{2,1,3,0:T(8,128)} copy(s32[2,96,128,32]{1,3,2,0:T(8,128)} %bitcast.10) | data formatting | bytes 6291456 | tf_op jit(solution)/shard_map/reshape | solution.py:223
  38.8 47.5 %fidelity.1.base = f32[2,96,4096]{2,1,0:T(8,128)} custom-call(f32[2,96,4096]{2,1,0:T(8,128)} %sky.3, f32[2,32,96,128]{3,2,1,0:T(8,128)} %bitcast.13, f32[2,32,96,128]{3,2,1,0:T(8,128)} %bitcast.14, s32[2,32,96,128]{3,2,1,0:T(8,128)} %bitcast.15, bf16[192,96]{1,0:T(8,128)(2,1)} %constant.34.clone.row_hi, bf16[192,96]{1,0:T(8,128)(2,1)} %constant.35.clone.row_lo, ...), custom_call_target="tpu_custom_call" | custom-call | tf_op jit(solution)/shard_map/fidelity/pallas_call | solution.py:234
  86.2 0.0 all-to-all-done.coef
  86.2 0.0 copy-start
  86.2 1.7 copy-done
  87.9 18.6 %prior.1 = (f32[2,96,4096]{2,1,0:T(8,128)}, f32[32,2,96,128]{3,2,1,0:T(8,128)}) custom-call(f32[32,2,96,128]{3,2,1,0:T(8,128)} %copy-done, f32[2,96,4096]{2,1,0:T(8,128)} %fidelity.1.base, f32[2,96,4096]{2,1,0:T(8,128)} %sky.3, bf16[256,256]{1,0:T(8,128)(2,1)} %constant.43.clone.synth2, bf16[128,256]{1,0:T(8,128)(2,1)} %constant.44.clone.synth_lo, ...), custom_call_target="tpu_custom_call" | custom-call | tf_op jit(solution)/shard_map/prior/pallas_call | solution.py:312
  106.5 77.1 %all_to_all.10 = f32[32,2,96,128]{3,2,1,0:T(8,128)} all-to-all(f32[32,2,96,128]{3,2,1,0:T(8,128)} %get-tuple-element.5), channel_id=1, replica_groups=mesh['groups'=1,'fac'=32] {'fac'}, dimensions={0} | all-to-all | bytes 6291456 | tf_op jit(solution)/shard_map/all_to_all | solution.py:360
  183.6 8.9 %shrink.1 = f32[64,96,128]{2,1,0:T(8,128)} custom-call(f32[64,96,128]{2,1,0:T(8,128)} %dual.1, f32[64,96,128]{2,1,0:T(8,128)} %bitcast.12), custom_call_target="tpu_custom_call" | custom-call | tf_op jit(solution)/shard_map/shrink/pallas_call | solution.py:341
Async XLA Ops:
  0.6 85.6 %all-to-all-start = ((f32[32,2,96,128]{3,2,1,0:T(8,128)}), f32[32,2,96,128]{3,2,1,0:T(8,128)S(1)}, u32[]{:S(2)}, u32[]{:S(2)}) async-start(f32[32,2,96,128]{3,2,1,0:T(8,128)} %bitcast.11), calls=%async_computation | async-start | bytes 6291456 | tf_op jit(solution)/shard_map/all_to_all | solution.py:357
  86.2 1.7 copy-start

commit v2 on v1

--- a/solution.py
+++ b/solution.py
@@ -171,17 +171,21 @@
 
     lax.fori_loop(0, rows // 8, slabs_forward, 0)
 
-    def lanes_both(slab, carry):
-        high, low = split(slab_part[slab])
+    group = 4
+
+    def lanes_both(index, carry):
+        pick = pl.ds(index * group, group)
+        high, low = split(slab_part[pick].reshape(group * rows, 2 * LANES))
         found = mul(high, lane_hi[...]) + mul(low, lane_hi[...]) + mul(high, lane_lo[...])
-        weight = mask[0, slab].astype(f32)
-        re = weight * (found[:, :LANES] - real[0, slab])
-        im = weight * (found[:, LANES:] - imag[0, slab])
+        weight = mask[0, pick].reshape(group * rows, LANES).astype(f32)
+        re = weight * (found[:, :LANES] - real[0, pick].reshape(group * rows, LANES))
+        im = weight * (found[:, LANES:] - imag[0, pick].reshape(group * rows, LANES))
         high, low = split(jnp.concatenate([re, im], 1))
-        slab_part[slab] = mul(high, inv_hi[...]) + mul(low, inv_hi[...]) + mul(high, inv_lo[...])
+        back = mul(high, inv_hi[...]) + mul(low, inv_hi[...]) + mul(high, inv_lo[...])
+        slab_part[pick] = back.reshape(group, rows, 2 * LANES)
         return carry
 
-    lax.fori_loop(0, slabs, lanes_both, 0)
+    lax.fori_loop(0, slabs // group, lanes_both, 0, unroll=True)
 
     def slabs_back(index, carry):
         start = pl.multiple_of(index * 8, 8)
@@ -211,6 +215,14 @@
     lax.fori_loop(0, columns // width, rows_back, 0)
 
 
+resident = pl.BlockSpec(memory_space=pltpu.VMEM)
+distant = pl.BlockSpec(memory_space=pltpu.HBM)
+
+
+def remote(array):
+    return pltpu.with_memory_space_constraint(array, pltpu.HBM)
+
+
 def whole(array):
     return pl.BlockSpec(array.shape, lambda *index: (0,) * array.ndim)
 
@@ -228,7 +240,7 @@
         *halves(forward), *halves(forward.T), *halves(lane), *halves(lane.T),
         twiddles(slabs, columns),
     )
-    tables = tuple(jnp.asarray(table) for table in tables)
+    tables = tuple(remote(jnp.asarray(table)) for table in tables)
     image = pl.BlockSpec((1, rows, columns), lambda c: (c, 0, 0))
     slab = pl.BlockSpec((1, slabs, rows, LANES), lambda c: (c, 0, 0, 0))
     return pl.pallas_call(
@@ -241,53 +253,80 @@
             pltpu.VMEM((2 * rows, columns), f32),
             pltpu.VMEM((slabs, rows, 2 * LANES), f32),
         ],
-        compiler_params=pltpu.CompilerParams(vmem_limit_bytes=56 << 20),
+        compiler_params=pltpu.CompilerParams(vmem_limit_bytes=32 << 20),
         name="fidelity",
-    )(sky, by_slab(real), by_slab(imag), by_slab(mask), *tables)
+    )(remote(sky), *(remote(by_slab(values)) for values in (real, imag, mask)), *tables)
 
 
 def prior_kernel(
-    coef, base, sky, synth2, synth_lo, rowt2, rowt_lo, row2, row_lo, ana2, ana_lo,
-    image, out, part_hi, part_lo, after,
+    coef, base_far, sky_far, synth2, synth_lo, rowt2, rowt_lo, row2, row_lo, ana2, ana_lo,
+    image, out, part, turned, held, base, sky, sems,
 ):
-    facets, rows, width = coef.shape[0], coef.shape[2], coef.shape[3]
-
-    def spread(facet):
-        high, low = split(coef[facet, 0])
-        return mul(jnp.concatenate([high, low], 1), synth2[...]) + mul(high, synth_lo[...])
-
-    before = spread(facets - 1)[:, width:]
-    for facet in range(facets):
-        both = spread(facet)
-        high, low = split(both[:, :width] + before)
-        before = both[:, width:]
-        lanes = slice(facet * width, (facet + 1) * width)
-        part_hi[:, lanes] = high
-        part_lo[:, lanes] = low
-
-    wide = 2 * width
-    for index in range(facets // 2):
-        lanes = slice(index * wide, (index + 1) * wide)
-        high, low = part_hi[:, lanes], part_lo[:, lanes]
-        step = mul(rowt2[...], jnp.concatenate([high, low], 0)) + mul(rowt_lo[...], high)
-        fresh = jnp.maximum(base[0, :, lanes] - step, 0.0)
-        image[0, :, lanes] = fresh
-        high, low = split(2.0 * fresh - sky[0, :, lanes])
-        turned = mul(row2[...], jnp.concatenate([high, low], 0)) + mul(row_lo[...], high)
-        high, low = split(turned)
-        for half in range(2):
-            facet = 2 * index + half
-            mine = slice(half * width, (half + 1) * width)
-            both = mul(
-                jnp.concatenate([high[:, mine], low[:, mine]], 1), ana2[...]
-            ) + mul(high[:, mine], ana_lo[...])
+    facets, channels, rows, width = coef.shape
+    columns = facets * width
+    wide = 4 * width
+    loads = []
+    for channel in range(channels):
+        loads.append((
+            pltpu.make_async_copy(base_far.at[channel], base.at[channel], sems.at[0, channel]),
+            pltpu.make_async_copy(sky_far.at[channel], sky.at[channel], sems.at[1, channel]),
+        ))
+        for copy in loads[-1]:
+            copy.start()
+    copies = []
+
+    for channel in range(channels):
+
+        def spread(facet):
+            high, low = split(coef[facet, channel])
+            return mul(jnp.concatenate([high, low], 1), synth2[...]) + mul(high, synth_lo[...])
+
+        before = spread(facets - 1)[:, width:]
+        for facet in range(facets):
+            both = spread(facet)
+            high, low = split(both[:, :width] + before)
+            before = both[:, width:]
+            lanes = slice(facet * width, (facet + 1) * width)
+            part[:rows, lanes] = high
+            part[rows:, lanes] = low
+
+        for copy in loads[channel]:
+            copy.wait()
+        for start in range(0, columns, wide):
+            lanes = slice(start, start + wide)
+            both = part[:, lanes]
+            step = mul(rowt2[...], both) + mul(rowt_lo[...], both[:rows])
+            fresh = jnp.maximum(base[channel, :, lanes] - step, 0.0)
+            base[channel, :, lanes] = fresh
+            high, low = split(2.0 * fresh - sky[channel, :, lanes])
+            part[:rows, lanes] = high
+            part[rows:, lanes] = low
+
+        copy = pltpu.make_async_copy(base.at[channel], image.at[channel], sems.at[2, channel])
+        copy.start()
+        copies.append(copy)
+
+        for start in range(0, columns, wide):
+            lanes = slice(start, start + wide)
+            both = part[:, lanes]
+            high, low = split(mul(row2[...], both) + mul(row_lo[...], both[:rows]))
+            for index in range(wide // width):
+                mine = slice(index * width, (index + 1) * width)
+                turned[start // width + index, :, :width] = high[:, mine]
+                turned[start // width + index, :, width:] = low[:, mine]
+
+        before = None
+        for facet in range(facets):
+            both = mul(turned[facet], ana2[...]) + mul(turned[facet, :, :width], ana_lo[...])
             if facet:
-                out[facet - 1, 0] = after[...] + both[:, width:]
-                after[...] = both[:, :width]
+                out[facet - 1, channel] = before + both[:, width:]
             else:
-                out[facets - 1, 0] = both[:, width:]
-                after[...] = both[:, :width]
-    out[facets - 1, 0] = after[...] + out[facets - 1, 0]
+                held[...] = both[:, width:]
+            before = both[:, :width]
+        out[facets - 1, channel] = before + held[...]
+
+    for copy in copies:
+        copy.wait()
 
 
 def prior(coefs, base, sky):
@@ -306,26 +345,26 @@
         np.concatenate([row[0], row[0]], 1), row[1],
         np.concatenate([analysis[0], analysis[0]], 0), analysis[1],
     )
-    tables = tuple(jnp.asarray(table) for table in tables)
-    image = pl.BlockSpec((1, rows, columns), lambda c: (c, 0, 0))
-    facet = pl.BlockSpec((facets, 1, rows, width), lambda c: (0, c, 0, 0))
+    tables = tuple(remote(jnp.asarray(table)) for table in tables)
     return pl.pallas_call(
         prior_kernel,
         out_shape=(
             jax.ShapeDtypeStruct(sky.shape, f32),
             jax.ShapeDtypeStruct(coefs.shape, f32),
         ),
-        grid=(channels,),
-        in_specs=[facet, image, image, *(whole(table) for table in tables)],
-        out_specs=(image, facet),
+        in_specs=[resident, distant, distant, *(whole(table) for table in tables)],
+        out_specs=(distant, resident),
         scratch_shapes=[
-            pltpu.VMEM((rows, columns), bf16),
-            pltpu.VMEM((rows, columns), bf16),
+            pltpu.VMEM((2 * rows, columns), bf16),
+            pltpu.VMEM((facets, rows, 2 * width), bf16),
             pltpu.VMEM((rows, width), f32),
+            pltpu.VMEM(sky.shape, f32),
+            pltpu.VMEM(sky.shape, f32),
+            pltpu.SemaphoreType.DMA((3, channels)),
         ],
-        compiler_params=pltpu.CompilerParams(vmem_limit_bytes=56 << 20),
+        compiler_params=pltpu.CompilerParams(vmem_limit_bytes=16 << 20),
         name="prior",
-    )(coefs, base, sky, *tables)
+    )(coefs, remote(base), remote(sky), *tables)
 
 
 def shrink_kernel(dual, change, out):
@@ -336,7 +375,7 @@
 
 def shrink(dual, change):
     channels, rows, width = dual.shape
-    step = 8
+    step = rows // 2
     block = pl.BlockSpec((channels, step, width), lambda r: (0, r, 0))
     return pl.pallas_call(
         shrink_kernel,
@@ -344,7 +383,7 @@
         grid=(rows // step,),
         in_specs=[block, block],
         out_specs=block,
-        compiler_params=pltpu.CompilerParams(vmem_limit_bytes=56 << 20),
+        compiler_params=pltpu.CompilerParams(vmem_limit_bytes=12 << 20),
         name="shrink",
     )(dual, change)
 

time: 193 us -> 166 us (0.86)
  Pallas kernels: 74.9 us -> 35.5 us
  waiting for transfers between devices: 0.01 us -> 14.6 us
  blocking collectives: 77.1 us -> 74.9 us
    pallas_call x1, Pallas kernels: 47.5 us -> 24.4 us  [fidelity(): pl.pallas_call(fidelity_kernel, out_shape=jax.ShapeDtypeStruct(sky.shape,...]
    all_to_all x1, waiting for transfers between devices: 0.01 us -> 14.6 us  [shards(): coefs = lax.all_to_all(sent, 'fac', split_axis=0, concat_axis=0, tiled=True)]
    pallas_call x1, Pallas kernels: 18.6 us -> 8.64 us  [prior(): pl.pallas_call(prior_kernel, out_shape=(jax.ShapeDtypeStruct(sky.shape, f...]
    pallas_call x1, Pallas kernels: 8.9 us -> 2.49 us  [shrink(): pl.pallas_call(shrink_kernel, out_shape=jax.ShapeDtypeStruct(dual.shape,...]
    all_to_all x1, blocking collectives: 77.1 us -> 74.9 us  [shards(): lax.all_to_all(change, 'fac', split_axis=0, concat_axis=0, tiled=True)]
    unnamed x5 -> x7, local copies, waits for them, and re-layouts: 17 us -> 17 us
  transfers between devices with their start and end apart: 1 -> 1, of which waited for: 0 -> 1; matrix products, arithmetic and copies ran while one was open for 16% -> 19% of each run, Pallas kernels for 25% -> 15%
where the time goes in v2:
time: 166 us; the launch traced here: 165 us
  blocking collectives  74.9 us (45%)
  Pallas kernels  35.5 us (21%)
  local copies, waits for them, and re-layouts  32.5 us (20%)
  waiting for transfers between devices  14.6 us (9%)
  starting transfers between devices  7.3 us (4%)
    all_to_all x1, blocking collectives, shards(): lax.all_to_all(change, 'fac', split_axis=0, concat_axis=0, tiled=True)  74.9 us
    pallas_call x1, Pallas kernels, fidelity(): pl.pallas_call(fidelity_kernel, out_shape=jax.ShapeDtypeStruct(sky.shape,...  24.4 us
    unnamed x7, local copies, waits for them, and re-layouts  17 us
    reshape x3, local copies, waits for them, and re-layouts, by_slab(): return values.reshape(channels, rows, LANES, slabs).transpose(0, 3, 1, 2)  15.5 us
    all_to_all x1, waiting for transfers between devices, shards(): coefs = lax.all_to_all(sent, 'fac', split_axis=0, concat_axis=0, tiled=True)  14.6 us
    pallas_call x1, Pallas kernels, prior(): pl.pallas_call(prior_kernel, out_shape=(jax.ShapeDtypeStruct(sky.shape, f...  8.64 us
    all_to_all x1, starting transfers between devices, shards(): coefs = lax.all_to_all(sent, 'fac', split_axis=0, concat_axis=0, tiled=True)  7.3 us
  transfers between devices with their start and end apart: 1, of which 1 were waited for; matrix products, arithmetic and copies ran while one was open for 19% of the time, Pallas kernels for 15%

profile of v2, /device:TPU:0, one launch (start us, length us, event | category | flops | bytes accessed | tf_op | source)
XLA Modules:
  0.0 165.5 jit_solution(18023830480091355575)
XLA Ops:
  0.6 7.3 %all-to-all-start = ((f32[32,2,96,128]{3,2,1,0:T(8,128)}), f32[32,2,96,128]{3,2,1,0:T(8,128)S(1)}, u32[]{:S(2)}, u32[]{:S(2)}) async-start(f32[32,2,96,128]{3,2,1,0:T(8,128)} %bitcast.8), calls=%async_computation | async-start | bytes 6291456 | tf_op jit(solution)/shard_map/all_to_all | solution.py:396
  7.9 5.1 %copy.24 = f32[2,96,4096]{1,2,0:T(8,128)} copy(f32[2,96,4096]{2,1,0:T(8,128)} %param.23) | data formatting | bytes 6291456 | tf_op args[1]
  13.1 5.1 %copy.25 = f32[2,96,128,32]{2,1,3,0:T(8,128)} copy(f32[2,96,128,32]{1,3,2,0:T(8,128)} %bitcast.10) | data formatting | bytes 6291456 | tf_op jit(solution)/shard_map/reshape | solution.py:235
  18.2 5.1 %copy.26 = f32[2,96,4096]{1,2,0:T(8,128)} copy(f32[2,96,4096]{2,1,0:T(8,128)} %param.24) | data formatting | bytes 6291456 | tf_op args[2]
  23.3 5.1 %copy.27 = f32[2,96,128,32]{2,1,3,0:T(8,128)} copy(f32[2,96,128,32]{1,3,2,0:T(8,128)} %bitcast.11) | data formatting | bytes 6291456 | tf_op jit(solution)/shard_map/reshape | solution.py:235
  28.4 5.1 %copy.28 = s32[2,96,4096]{1,2,0:T(8,128)} copy(s32[2,96,4096]{2,1,0:T(8,128)} %param.25) | data formatting | bytes 6291456 | tf_op args[3]
  33.6 5.2 %copy.29 = s32[2,96,128,32]{2,1,3,0:T(8,128)} copy(s32[2,96,128,32]{1,3,2,0:T(8,128)} %bitcast.12) | data formatting | bytes 6291456 | tf_op jit(solution)/shard_map/reshape | solution.py:235
  38.7 24.4 %fidelity.1.base_far = f32[2,96,4096]{2,1,0:T(8,128)S(1)} custom-call(f32[2,96,4096]{2,1,0:T(8,128)} %sky_far.1, f32[2,32,96,128]{3,2,1,0:T(8,128)} %bitcast.13, f32[2,32,96,128]{3,2,1,0:T(8,128)} %bitcast.14, s32[2,32,96,128]{3,2,1,0:T(8,128)} %bitcast.15, bf16[192,96]{1,0:T(8,128)(2,1)} %constant.34.clone.row_hi, bf16[192,96]{1,0:T(8,128)(2,1)} %constant.35.clone.row_lo, ...), custom_call_target="tpu_custom_call" | custom-call | tf_op jit(solution)/shard_map/fidelity/pallas_call | solution.py:246
  63.1 0.0 copy-start.1
  63.1 1.7 %copy-done.1 = f32[2,96,4096]{2,1,0:T(8,128)} copy-done((f32[2,96,4096]{2,1,0:T(8,128)}, f32[2,96,4096]{2,1,0:T(8,128)S(1)}, u32[]{:S(2)}) %copy-start.1) | copy-done | bytes 3145752
  64.8 14.6 %all-to-all-done.coef = f32[32,2,96,128]{3,2,1,0:T(8,128)S(1)} async-done(((f32[32,2,96,128]{3,2,1,0:T(8,128)}), f32[32,2,96,128]{3,2,1,0:T(8,128)S(1)}, u32[]{:S(2)}, u32[]{:S(2)}) %all-to-all-start) | async-done | bytes 3145760 | tf_op jit(solution)/shard_map/all_to_all | solution.py:396
  79.4 8.6 %prior.1 = (f32[2,96,4096]{2,1,0:T(8,128)}, f32[32,2,96,128]{3,2,1,0:T(8,128)S(1)}) custom-call(f32[32,2,96,128]{3,2,1,0:T(8,128)S(1)} %all-to-all-done.coef, f32[2,96,4096]{2,1,0:T(8,128)} %copy-done.1, f32[2,96,4096]{2,1,0:T(8,128)} %sky_far.1, bf16[256,256]{1,0:T(8,128)(2,1)} %constant.43.clone.synth2, bf16[128,256]{1,0:T(8,128)(2,1)} %constant.44.clone.synth_lo, ...), custom_call_target="tpu_custom_call" | custom-call | tf_op jit(solution)/shard_map/prior/pallas_call | solution.py:349
  88.0 0.0 copy-start
  88.1 74.9 %all_to_all.10 = f32[32,2,96,128]{3,2,1,0:T(8,128)S(1)} all-to-all(f32[32,2,96,128]{3,2,1,0:T(8,128)S(1)} %get-tuple-element.5), channel_id=1, replica_groups=mesh['groups'=1,'fac'=32] {'fac'}, dimensions={0} | all-to-all | bytes 6291456 | tf_op jit(solution)/shard_map/all_to_all | solution.py:399
  163.0 0.0 copy-done
  163.0 2.5 %shrink.1 = f32[64,96,128]{2,1,0:T(8,128)} custom-call(f32[64,96,128]{2,1,0:T(8,128)S(1)} %copy-done, f32[64,96,128]{2,1,0:T(8,128)S(1)} %bitcast.9), custom_call_target="tpu_custom_call" | custom-call | tf_op jit(solution)/shard_map/shrink/pallas_call | solution.py:380
Async XLA Ops:
  0.6 78.8 %all-to-all-start = ((f32[32,2,96,128]{3,2,1,0:T(8,128)}), f32[32,2,96,128]{3,2,1,0:T(8,128)S(1)}, u32[]{:S(2)}, u32[]{:S(2)}) async-start(f32[32,2,96,128]{3,2,1,0:T(8,128)} %bitcast.8), calls=%async_computation | async-start | bytes 6291456 | tf_op jit(solution)/shard_map/all_to_all | solution.py:396
  63.1 1.7 %copy-start.1 = (f32[2,96,4096]{2,1,0:T(8,128)}, f32[2,96,4096]{2,1,0:T(8,128)S(1)}, u32[]{:S(2)}) copy-start(f32[2,96,4096]{2,1,0:T(8,128)S(1)} %fidelity.1.base_far) | copy-start | bytes 9437188
  88.0 74.9 %copy-start = (f32[64,96,128]{2,1,0:T(8,128)S(1)}, f32[64,96,128]{2,1,0:T(8,128)}, u32[]{:S(2)}) copy-start(f32[64,96,128]{2,1,0:T(8,128)} %dual.1) | copy-start | bytes 9437188

commit v3 on v2

--- a/solution.py
+++ b/solution.py
@@ -258,71 +258,100 @@
     )(remote(sky), *(remote(by_slab(values)) for values in (real, imag, mask)), *tables)
 
 
-def prior_kernel(
-    coef, base_far, sky_far, synth2, synth_lo, rowt2, rowt_lo, row2, row_lo, ana2, ana_lo,
-    image, out, part, turned, held, base, sky, sems,
-):
+def prior_kernel(*refs):
+    coef, base_far, sky_far = refs[:3]
+    tables_far, tables = refs[3:11], refs[13:21]
+    image, out = refs[11:13]
+    part, turned, held, base, sky, sems, table_sems = refs[21:]
+    synth2, synth_lo, rowt2, rowt_lo, row2, row_lo, ana2, ana_lo = tables
     facets, channels, rows, width = coef.shape
     columns = facets * width
     wide = 4 * width
-    loads = []
-    for channel in range(channels):
-        loads.append((
+    batch = 4
+
+    fetches = [
+        pltpu.make_async_copy(tables_far[index], tables[index], table_sems.at[index])
+        for index in range(len(tables))
+    ]
+    loads = [
+        (
             pltpu.make_async_copy(base_far.at[channel], base.at[channel], sems.at[0, channel]),
             pltpu.make_async_copy(sky_far.at[channel], sky.at[channel], sems.at[1, channel]),
-        ))
-        for copy in loads[-1]:
-            copy.start()
+        )
+        for channel in range(channels)
+    ]
+    for copy in (*fetches[:2], *loads[0], *fetches[2:]):
+        copy.start()
     copies = []
 
+    for copy in fetches[:2]:
+        copy.wait()
     for channel in range(channels):
 
-        def spread(facet):
-            high, low = split(coef[facet, channel])
-            return mul(jnp.concatenate([high, low], 1), synth2[...]) + mul(high, synth_lo[...])
-
-        before = spread(facets - 1)[:, width:]
-        for facet in range(facets):
-            both = spread(facet)
-            high, low = split(both[:, :width] + before)
-            before = both[:, width:]
-            lanes = slice(facet * width, (facet + 1) * width)
-            part[:rows, lanes] = high
-            part[rows:, lanes] = low
-
+        before = None
+        for first in range(0, facets, batch):
+            high, low = split(coef[first : first + batch, channel].reshape(batch * rows, width))
+            both = mul(jnp.concatenate([high, low], 1), synth2[...]) + mul(high, synth_lo[...])
+            for index in range(batch):
+                facet = first + index
+                mine = both[index * rows : (index + 1) * rows]
+                if facet:
+                    high, low = split(mine[:, :width] + before)
+                    lanes = slice(facet * width, (facet + 1) * width)
+                    part[channel, :rows, lanes] = high
+                    part[channel, rows:, lanes] = low
+                else:
+                    held[...] = mine[:, :width]
+                before = mine[:, width:]
+        high, low = split(held[...] + before)
+        part[channel, :rows, :width] = high
+        part[channel, rows:, :width] = low
+
+    for copy in fetches[2:4]:
+        copy.wait()
+    for channel in range(channels):
         for copy in loads[channel]:
             copy.wait()
+        if channel + 1 < channels:
+            for copy in loads[channel + 1]:
+                copy.start()
         for start in range(0, columns, wide):
             lanes = slice(start, start + wide)
-            both = part[:, lanes]
+            both = part[channel, :, lanes]
             step = mul(rowt2[...], both) + mul(rowt_lo[...], both[:rows])
             fresh = jnp.maximum(base[channel, :, lanes] - step, 0.0)
             base[channel, :, lanes] = fresh
             high, low = split(2.0 * fresh - sky[channel, :, lanes])
-            part[:rows, lanes] = high
-            part[rows:, lanes] = low
-
+            part[channel, :rows, lanes] = high
+            part[channel, rows:, lanes] = low
         copy = pltpu.make_async_copy(base.at[channel], image.at[channel], sems.at[2, channel])
         copy.start()
         copies.append(copy)
 
+        if channel == 0:
+            for copy in fetches[4:]:
+                copy.wait()
         for start in range(0, columns, wide):
             lanes = slice(start, start + wide)
-            both = part[:, lanes]
+            both = part[channel, :, lanes]
             high, low = split(mul(row2[...], both) + mul(row_lo[...], both[:rows]))
             for index in range(wide // width):
                 mine = slice(index * width, (index + 1) * width)
-                turned[start // width + index, :, :width] = high[:, mine]
-                turned[start // width + index, :, width:] = low[:, mine]
+                turned[channel, start // width + index, :, :width] = high[:, mine]
+                turned[channel, start // width + index, :, width:] = low[:, mine]
 
         before = None
-        for facet in range(facets):
-            both = mul(turned[facet], ana2[...]) + mul(turned[facet, :, :width], ana_lo[...])
-            if facet:
-                out[facet - 1, channel] = before + both[:, width:]
-            else:
-                held[...] = both[:, width:]
-            before = both[:, :width]
+        for first in range(0, facets, batch):
+            values = turned[channel, first : first + batch].reshape(batch * rows, 2 * width)
+            both = mul(values, ana2[...]) + mul(values[:, :width], ana_lo[...])
+            for index in range(batch):
+                facet = first + index
+                mine = both[index * rows : (index + 1) * rows]
+                if facet:
+                    out[facet - 1, channel] = before + mine[:, width:]
+                else:
+                    held[...] = mine[:, width:]
+                before = mine[:, :width]
         out[facets - 1, channel] = before + held[...]
 
     for copy in copies:
@@ -352,38 +381,51 @@
             jax.ShapeDtypeStruct(sky.shape, f32),
             jax.ShapeDtypeStruct(coefs.shape, f32),
         ),
-        in_specs=[resident, distant, distant, *(whole(table) for table in tables)],
+        in_specs=[resident, distant, distant, *(distant for table in tables)],
         out_specs=(distant, resident),
         scratch_shapes=[
-            pltpu.VMEM((2 * rows, columns), bf16),
-            pltpu.VMEM((facets, rows, 2 * width), bf16),
+            *(pltpu.VMEM(table.shape, bf16) for table in tables),
+            pltpu.VMEM((channels, 2 * rows, columns), bf16),
+            pltpu.VMEM((channels, facets, rows, 2 * width), bf16),
             pltpu.VMEM((rows, width), f32),
             pltpu.VMEM(sky.shape, f32),
             pltpu.VMEM(sky.shape, f32),
             pltpu.SemaphoreType.DMA((3, channels)),
+            pltpu.SemaphoreType.DMA((len(tables),)),
         ],
-        compiler_params=pltpu.CompilerParams(vmem_limit_bytes=16 << 20),
+        compiler_params=pltpu.CompilerParams(vmem_limit_bytes=20 << 20),
         name="prior",
     )(coefs, remote(base), remote(sky), *tables)
 
 
-def shrink_kernel(dual, change, out):
-    lifted = dual[...] + change[...]
-    norm = jnp.sqrt(jnp.sum(lifted * lifted, 0))
-    out[...] = lifted * (1.0 / jnp.maximum(1.0, norm / ball_radius))[None]
+def shrink_kernel(dual, change, out_far, out, sems):
+    channels = dual.shape[0]
+    some = channels // sems.shape[0]
+    total = 0.0
+    for channel in range(channels):
+        lifted = dual[channel] + change[channel]
+        total = total + lifted * lifted
+    scale = 1.0 / jnp.maximum(1.0, jnp.sqrt(total) / ball_radius)
+    copies = []
+    for first in range(0, channels, some):
+        for channel in range(first, first + some):
+            out[channel] = (dual[channel] + change[channel]) * scale
+        pick = pl.ds(first, some)
+        copy = pltpu.make_async_copy(out.at[pick], out_far.at[pick], sems.at[first // some])
+        copy.start()
+        copies.append(copy)
+    for copy in copies:
+        copy.wait()
 
 
 def shrink(dual, change):
-    channels, rows, width = dual.shape
-    step = rows // 2
-    block = pl.BlockSpec((channels, step, width), lambda r: (0, r, 0))
     return pl.pallas_call(
         shrink_kernel,
         out_shape=jax.ShapeDtypeStruct(dual.shape, f32),
-        grid=(rows // step,),
-        in_specs=[block, block],
-        out_specs=block,
-        compiler_params=pltpu.CompilerParams(vmem_limit_bytes=12 << 20),
+        in_specs=[resident, resident],
+        out_specs=distant,
+        scratch_shapes=[pltpu.VMEM(dual.shape, f32), pltpu.SemaphoreType.DMA((8,))],
+        compiler_params=pltpu.CompilerParams(vmem_limit_bytes=6 << 20),
         name="shrink",
     )(dual, change)
 

time: 166 us -> 165 us (level)
  no operation moved by 1% of the time
where the time goes in v3:
time: 165 us; the launch traced here: 164 us
  blocking collectives  74.9 us (45%)
  Pallas kernels  34.1 us (21%)
  local copies, waits for them, and re-layouts  32.5 us (20%)
  waiting for transfers between devices  14.6 us (9%)
  starting transfers between devices  7.3 us (4%)
    all_to_all x1, blocking collectives, shards(): lax.all_to_all(change, 'fac', split_axis=0, concat_axis=0, tiled=True)  74.9 us
    pallas_call x1, Pallas kernels, fidelity(): pl.pallas_call(fidelity_kernel, out_shape=jax.ShapeDtypeStruct(sky.shape,...  24.4 us
    unnamed x7, local copies, waits for them, and re-layouts  17 us
    reshape x3, local copies, waits for them, and re-layouts, by_slab(): return values.reshape(channels, rows, LANES, slabs).transpose(0, 3, 1, 2)  15.5 us
    all_to_all x1, waiting for transfers between devices, shards(): coefs = lax.all_to_all(sent, 'fac', split_axis=0, concat_axis=0, tiled=True)  14.6 us
    all_to_all x1, starting transfers between devices, shards(): coefs = lax.all_to_all(sent, 'fac', split_axis=0, concat_axis=0, tiled=True)  7.3 us
    pallas_call x1, Pallas kernels, prior(): pl.pallas_call(prior_kernel, out_shape=(jax.ShapeDtypeStruct(sky.shape, f...  7.21 us
  transfers between devices with their start and end apart: 1, of which 1 were waited for; matrix products, arithmetic and copies ran while one was open for 19% of the time, Pallas kernels for 15%

profile of v3, /device:TPU:0, one launch (start us, length us, event | category | flops | bytes accessed | tf_op | source)
XLA Modules:
  0.0 164.1 jit_solution(8539675111913801159)
XLA Ops:
  0.6 7.3 %all-to-all-start = ((f32[32,2,96,128]{3,2,1,0:T(8,128)}), f32[32,2,96,128]{3,2,1,0:T(8,128)S(1)}, u32[]{:S(2)}, u32[]{:S(2)}) async-start(f32[32,2,96,128]{3,2,1,0:T(8,128)} %bitcast.8), calls=%async_computation | async-start | bytes 6291456 | tf_op jit(solution)/shard_map/all_to_all | solution.py:438
  7.9 5.1 %copy.24 = f32[2,96,4096]{1,2,0:T(8,128)} copy(f32[2,96,4096]{2,1,0:T(8,128)} %param.23) | data formatting | bytes 6291456 | tf_op args[1]
  13.1 5.1 %copy.25 = f32[2,96,128,32]{2,1,3,0:T(8,128)} copy(f32[2,96,128,32]{1,3,2,0:T(8,128)} %bitcast.10) | data formatting | bytes 6291456 | tf_op jit(solution)/shard_map/reshape | solution.py:235
  18.2 5.1 %copy.26 = f32[2,96,4096]{1,2,0:T(8,128)} copy(f32[2,96,4096]{2,1,0:T(8,128)} %param.24) | data formatting | bytes 6291456 | tf_op args[2]
  23.3 5.1 %copy.27 = f32[2,96,128,32]{2,1,3,0:T(8,128)} copy(f32[2,96,128,32]{1,3,2,0:T(8,128)} %bitcast.11) | data formatting | bytes 6291456 | tf_op jit(solution)/shard_map/reshape | solution.py:235
  28.4 5.1 %copy.28 = s32[2,96,4096]{1,2,0:T(8,128)} copy(s32[2,96,4096]{2,1,0:T(8,128)} %param.25) | data formatting | bytes 6291456 | tf_op args[3]
  33.6 5.2 %copy.29 = s32[2,96,128,32]{2,1,3,0:T(8,128)} copy(s32[2,96,128,32]{1,3,2,0:T(8,128)} %bitcast.12) | data formatting | bytes 6291456 | tf_op jit(solution)/shard_map/reshape | solution.py:235
  38.7 24.4 %fidelity.1.refs_1_ = f32[2,96,4096]{2,1,0:T(8,128)S(1)} custom-call(f32[2,96,4096]{2,1,0:T(8,128)} %refs_2_.1, f32[2,32,96,128]{3,2,1,0:T(8,128)} %bitcast.13, f32[2,32,96,128]{3,2,1,0:T(8,128)} %bitcast.14, s32[2,32,96,128]{3,2,1,0:T(8,128)} %bitcast.15, bf16[192,96]{1,0:T(8,128)(2,1)} %constant.34.clone.row_hi, bf16[192,96]{1,0:T(8,128)(2,1)} %constant.35.clone.row_lo, ...), custom_call_target="tpu_custom_call" | custom-call | tf_op jit(solution)/shard_map/fidelity/pallas_call | solution.py:246
  63.1 0.0 copy-start.1
  63.1 1.7 %copy-done.1 = f32[2,96,4096]{2,1,0:T(8,128)} copy-done((f32[2,96,4096]{2,1,0:T(8,128)}, f32[2,96,4096]{2,1,0:T(8,128)S(1)}, u32[]{:S(2)}) %copy-start.1) | copy-done | bytes 3145752
  64.8 14.6 %all-to-all-done.refs_0_ = f32[32,2,96,128]{3,2,1,0:T(8,128)S(1)} async-done(((f32[32,2,96,128]{3,2,1,0:T(8,128)}), f32[32,2,96,128]{3,2,1,0:T(8,128)S(1)}, u32[]{:S(2)}, u32[]{:S(2)}) %all-to-all-start) | async-done | bytes 3145760 | tf_op jit(solution)/shard_map/all_to_all | solution.py:438
  79.4 7.2 %prior.1 = (f32[2,96,4096]{2,1,0:T(8,128)}, f32[32,2,96,128]{3,2,1,0:T(8,128)S(1)}) custom-call(f32[32,2,96,128]{3,2,1,0:T(8,128)S(1)} %all-to-all-done.refs_0_, f32[2,96,4096]{2,1,0:T(8,128)} %copy-done.1, f32[2,96,4096]{2,1,0:T(8,128)} %refs_2_.1, bf16[256,256]{1,0:T(8,128)(2,1)} %constant.43.clone.refs_3_, bf16[128,256]{1,0:T(8,128)(2,1)} %constant.44.clone.refs_4_, ...), custom_call_target="tpu_custom_call" | custom-call | tf_op jit(solution)/shard_map/prior/pallas_call | solution.py:378
  86.6 0.0 copy-start
  86.6 74.9 %all_to_all.10 = f32[32,2,96,128]{3,2,1,0:T(8,128)S(1)} all-to-all(f32[32,2,96,128]{3,2,1,0:T(8,128)S(1)} %get-tuple-element.5), channel_id=1, replica_groups=mesh['groups'=1,'fac'=32] {'fac'}, dimensions={0} | all-to-all | bytes 6291456 | tf_op jit(solution)/shard_map/all_to_all | solution.py:441
  161.6 0.0 copy-done
  161.6 2.5 %shrink.1 = f32[64,96,128]{2,1,0:T(8,128)} custom-call(f32[64,96,128]{2,1,0:T(8,128)S(1)} %copy-done, f32[64,96,128]{2,1,0:T(8,128)S(1)} %bitcast.9), custom_call_target="tpu_custom_call" | custom-call | tf_op jit(solution)/shard_map/shrink/pallas_call | solution.py:422
Async XLA Ops:
  0.6 78.8 %all-to-all-start = ((f32[32,2,96,128]{3,2,1,0:T(8,128)}), f32[32,2,96,128]{3,2,1,0:T(8,128)S(1)}, u32[]{:S(2)}, u32[]{:S(2)}) async-start(f32[32,2,96,128]{3,2,1,0:T(8,128)} %bitcast.8), calls=%async_computation | async-start | bytes 6291456 | tf_op jit(solution)/shard_map/all_to_all | solution.py:438
  63.1 1.7 %copy-start.1 = (f32[2,96,4096]{2,1,0:T(8,128)}, f32[2,96,4096]{2,1,0:T(8,128)S(1)}, u32[]{:S(2)}) copy-start(f32[2,96,4096]{2,1,0:T(8,128)S(1)} %fidelity.1.refs_1_) | copy-start | bytes 9437188
  86.6 74.9 %copy-start = (f32[64,96,128]{2,1,0:T(8,128)S(1)}, f32[64,96,128]{2,1,0:T(8,128)}, u32[]{:S(2)}) copy-start(f32[64,96,128]{2,1,0:T(8,128)} %dual.1) | copy-start | bytes 9437188

commit v4 on v3

--- a/solution.py
+++ b/solution.py
@@ -139,11 +139,18 @@
 
 def fidelity_kernel(
     sky, real, imag, mask, row_hi, row_lo, back_hi, back_lo, lane_hi, lane_lo,
-    inv_hi, inv_lo, twist, base, row_part, slab_part,
+    inv_hi, inv_lo, twist, early_far, base, early, row_part, slab_part, sem,
 ):
     rows, columns = sky.shape[1], sky.shape[2]
     slabs = columns // LANES
     width = 512
+
+    @pl.when(pl.program_id(0) == 0)
+    def fetch():
+        copy = pltpu.make_async_copy(early_far, early, sem)
+        copy.start()
+        copy.wait()
+
 
     def rows_forward(index, carry):
         lanes = pl.ds(pl.multiple_of(index * width, width), width)
@@ -227,7 +234,7 @@
     return pl.BlockSpec(array.shape, lambda *index: (0,) * array.ndim)
 
 
-def fidelity(sky, real, imag, mask):
+def fidelity(sky, real, imag, mask, early):
     channels, rows, columns = sky.shape
     slabs = columns // LANES
 
@@ -245,30 +252,37 @@
     slab = pl.BlockSpec((1, slabs, rows, LANES), lambda c: (c, 0, 0, 0))
     return pl.pallas_call(
         fidelity_kernel,
-        out_shape=jax.ShapeDtypeStruct(sky.shape, f32),
+        out_shape=(
+            jax.ShapeDtypeStruct(sky.shape, f32),
+            jax.ShapeDtypeStruct(early.shape, early.dtype),
+        ),
         grid=(channels,),
-        in_specs=[image, slab, slab, slab, *(whole(table) for table in tables)],
-        out_specs=image,
+        in_specs=[image, slab, slab, slab, *(whole(table) for table in tables), distant],
+        out_specs=(image, resident),
         scratch_shapes=[
             pltpu.VMEM((2 * rows, columns), f32),
             pltpu.VMEM((slabs, rows, 2 * LANES), f32),
+            pltpu.SemaphoreType.DMA,
         ],
         compiler_params=pltpu.CompilerParams(vmem_limit_bytes=32 << 20),
         name="fidelity",
-    )(remote(sky), *(remote(by_slab(values)) for values in (real, imag, mask)), *tables)
+    )(remote(sky), *(remote(by_slab(values)) for values in (real, imag, mask)), *tables, remote(early))
 
 
 def prior_kernel(*refs):
-    coef, base_far, sky_far = refs[:3]
-    tables_far, tables = refs[3:11], refs[13:21]
-    image, out = refs[11:13]
-    part, turned, held, base, sky, sems, table_sems = refs[21:]
-    synth2, synth_lo, rowt2, rowt_lo, row2, row_lo, ana2, ana_lo = tables
+    coef, base_far, sky_far, kept = refs[:4]
+    tables_far, tables = refs[4:10], refs[12:18]
+    image, out = refs[10:12]
+    part, turned, held, base, sky, sems, table_sems, synth = refs[18:]
+    rowt2, rowt_lo, row2, row_lo, ana2, ana_lo = tables
     facets, channels, rows, width = coef.shape
+    synth2, synth_lo = synth.at[: 2 * width], synth.at[2 * width :]
     columns = facets * width
     wide = 4 * width
     batch = 4
 
+    first_table = pltpu.make_async_copy(kept, synth, table_sems.at[len(tables)])
+    first_table.start()
     fetches = [
         pltpu.make_async_copy(tables_far[index], tables[index], table_sems.at[index])
         for index in range(len(tables))
@@ -280,12 +294,11 @@
         )
         for channel in range(channels)
     ]
-    for copy in (*fetches[:2], *loads[0], *fetches[2:]):
+    for copy in (*fetches[:2], *loads[0], *fetches[2:], *loads[1]):
         copy.start()
     copies = []
 
-    for copy in fetches[:2]:
-        copy.wait()
+    first_table.wait()
     for channel in range(channels):
 
         before = None
@@ -307,14 +320,11 @@
         part[channel, :rows, :width] = high
         part[channel, rows:, :width] = low
 
-    for copy in fetches[2:4]:
+    for copy in fetches[:2]:
         copy.wait()
     for channel in range(channels):
         for copy in loads[channel]:
             copy.wait()
-        if channel + 1 < channels:
-            for copy in loads[channel + 1]:
-                copy.start()
         for start in range(0, columns, wide):
             lanes = slice(start, start + wide)
             both = part[channel, :, lanes]
@@ -329,7 +339,7 @@
         copies.append(copy)
 
         if channel == 0:
-            for copy in fetches[4:]:
+            for copy in fetches[2:]:
                 copy.wait()
         for start in range(0, columns, wide):
             lanes = slice(start, start + wide)
@@ -358,18 +368,22 @@
         copy.wait()
 
 
-def prior(coefs, base, sky):
+def synthesis_table(width):
+    facet_table = facet_wavelet(width)
+    own, other = facet_table[:, :width], facet_table[:, width:]
+    high, low = halves(np.concatenate([own.T, other.T], 1))
+    return jnp.asarray(np.concatenate([high, high, low], 0))
+
+
+def prior(coefs, base, sky, synth):
     channels, rows, columns = sky.shape
     facets, width = coefs.shape[0], coefs.shape[3]
     facet_table = facet_wavelet(width)
-    own, other = facet_table[:, :width], facet_table[:, width:]
-    synth = halves(np.concatenate([own.T, other.T], 1))
     analysis = halves(dual_step * facet_table)
     row_table = row_wavelet(rows)
     rowt = halves(primal_step * row_table.T)
     row = halves(row_table)
     tables = (
-        np.concatenate([synth[0], synth[0]], 0), synth[1],
         np.concatenate([rowt[0], rowt[0]], 1), rowt[1],
         np.concatenate([row[0], row[0]], 1), row[1],
         np.concatenate([analysis[0], analysis[0]], 0), analysis[1],
@@ -381,7 +395,7 @@
             jax.ShapeDtypeStruct(sky.shape, f32),
             jax.ShapeDtypeStruct(coefs.shape, f32),
         ),
-        in_specs=[resident, distant, distant, *(distant for table in tables)],
+        in_specs=[resident, distant, distant, resident, *(distant for table in tables)],
         out_specs=(distant, resident),
         scratch_shapes=[
             *(pltpu.VMEM(table.shape, bf16) for table in tables),
@@ -391,11 +405,12 @@
             pltpu.VMEM(sky.shape, f32),
             pltpu.VMEM(sky.shape, f32),
             pltpu.SemaphoreType.DMA((3, channels)),
-            pltpu.SemaphoreType.DMA((len(tables),)),
+            pltpu.SemaphoreType.DMA((len(tables) + 1,)),
+            pltpu.VMEM(synth.shape, bf16),
         ],
         compiler_params=pltpu.CompilerParams(vmem_limit_bytes=20 << 20),
         name="prior",
-    )(coefs, remote(base), remote(sky), *tables)
+    )(coefs, remote(base), remote(sky), synth, *tables)
 
 
 def shrink_kernel(dual, change, out_far, out, sems):
@@ -436,8 +451,10 @@
     width = column_count // facets
     sent = dual_field.reshape(facets, channels, row_count, width)
     coefs = lax.all_to_all(sent, "fac", split_axis=0, concat_axis=0, tiled=True)
-    base = fidelity(sky_image, measured_real, measured_imaginary, sampling_mask)
-    next_image, change = prior(coefs, base, sky_image)
+    base, synth = fidelity(
+        sky_image, measured_real, measured_imaginary, sampling_mask, synthesis_table(width)
+    )
+    next_image, change = prior(coefs, base, sky_image, synth)
     change = lax.all_to_all(change, "fac", split_axis=0, concat_axis=0, tiled=True)
     next_dual = shrink(dual_field, change.reshape(dual_field.shape))
     return (next_image, next_dual)

time: 165 us -> 164 us (level)
  transfers between devices with their start and end apart: 1 -> 1, of which waited for: 1 -> 1; matrix products, arithmetic and copies ran while one was open for 19% -> 19% of each run, Pallas kernels for 15% -> 16%
where the time goes in v4:
time: 164 us; the launch traced here: 163 us
  blocking collectives  74.9 us (46%)
  Pallas kernels  34.8 us (21%)
  local copies, waits for them, and re-layouts  32.4 us (20%)
  waiting for transfers between devices  13 us (8%)
  starting transfers between devices  7.3 us (4%)
    all_to_all x1, blocking collectives, shards(): lax.all_to_all(change, 'fac', split_axis=0, concat_axis=0, tiled=True)  74.9 us
    pallas_call x1, Pallas kernels, fidelity(): pl.pallas_call(fidelity_kernel, out_shape=(jax.ShapeDtypeStruct(sky.shape...  26 us
    unnamed x7, local copies, waits for them, and re-layouts  17 us
    reshape x3, local copies, waits for them, and re-layouts, by_slab(): return values.reshape(channels, rows, LANES, slabs).transpose(0, 3, 1, 2)  15.5 us
    all_to_all x1, waiting for transfers between devices, shards(): coefs = lax.all_to_all(sent, 'fac', split_axis=0, concat_axis=0, tiled=True)  13 us
    all_to_all x1, starting transfers between devices, shards(): coefs = lax.all_to_all(sent, 'fac', split_axis=0, concat_axis=0, tiled=True)  7.3 us
    pallas_call x1, Pallas kernels, prior(): pl.pallas_call(prior_kernel, out_shape=(jax.ShapeDtypeStruct(sky.shape, f...  6.25 us
  transfers between devices with their start and end apart: 1, of which 1 were waited for; matrix products, arithmetic and copies ran while one was open for 19% of the time, Pallas kernels for 16%

profile of v4, /device:TPU:0, one launch (start us, length us, event | category | flops | bytes accessed | tf_op | source)
XLA Modules:
  0.0 163.1 jit_solution(13816017945510673703)
XLA Ops:
  0.6 7.3 %all-to-all-start = ((f32[32,2,96,128]{3,2,1,0:T(8,128)}), f32[32,2,96,128]{3,2,1,0:T(8,128)S(1)}, u32[]{:S(2)}, u32[]{:S(2)}) async-start(f32[32,2,96,128]{3,2,1,0:T(8,128)} %bitcast.8), calls=%async_computation | async-start | bytes 6291456 | tf_op jit(solution)/shard_map/all_to_all | solution.py:453
  7.9 5.1 %copy.23 = f32[2,96,4096]{1,2,0:T(8,128)} copy(f32[2,96,4096]{2,1,0:T(8,128)} %param.22) | data formatting | bytes 6291456 | tf_op args[1]
  13.1 5.1 %copy.24 = f32[2,96,128,32]{2,1,3,0:T(8,128)} copy(f32[2,96,128,32]{1,3,2,0:T(8,128)} %bitcast.10) | data formatting | bytes 6291456 | tf_op jit(solution)/shard_map/reshape | solution.py:242
  18.2 5.1 %copy.25 = f32[2,96,4096]{1,2,0:T(8,128)} copy(f32[2,96,4096]{2,1,0:T(8,128)} %param.23) | data formatting | bytes 6291456 | tf_op args[2]
  23.3 5.1 %copy.26 = f32[2,96,128,32]{2,1,3,0:T(8,128)} copy(f32[2,96,128,32]{1,3,2,0:T(8,128)} %bitcast.11) | data formatting | bytes 6291456 | tf_op jit(solution)/shard_map/reshape | solution.py:242
  28.4 5.1 %copy.27 = s32[2,96,4096]{1,2,0:T(8,128)} copy(s32[2,96,4096]{2,1,0:T(8,128)} %param.24) | data formatting | bytes 6291456 | tf_op args[3]
  33.5 5.2 %copy.28 = s32[2,96,128,32]{2,1,3,0:T(8,128)} copy(s32[2,96,128,32]{1,3,2,0:T(8,128)} %bitcast.12) | data formatting | bytes 6291456 | tf_op jit(solution)/shard_map/reshape | solution.py:242
  38.7 26.0 %fidelity.1 = (f32[2,96,4096]{2,1,0:T(8,128)S(1)}, bf16[384,256]{1,0:T(8,128)(2,1)S(1)}) custom-call(f32[2,96,4096]{2,1,0:T(8,128)} %refs_2_.1, f32[2,32,96,128]{3,2,1,0:T(8,128)} %bitcast.13, f32[2,32,96,128]{3,2,1,0:T(8,128)} %bitcast.14, s32[2,32,96,128]{3,2,1,0:T(8,128)} %bitcast.15, bf16[192,96]{1,0:T(8,128)(2,1)} %constant.33.clone.row_hi, ...), custom_call_target="tpu_custom_call" | custom-call | tf_op jit(solution)/shard_map/fidelity/pallas_call | solution.py:253
  64.7 0.0 copy-start.1
  64.7 1.7 %copy-done.1 = f32[2,96,4096]{2,1,0:T(8,128)} copy-done((f32[2,96,4096]{2,1,0:T(8,128)}, f32[2,96,4096]{2,1,0:T(8,128)S(1)}, u32[]{:S(2)}) %copy-start.1) | copy-done | bytes 3145752
  66.4 13.0 %all-to-all-done.refs_0_ = f32[32,2,96,128]{3,2,1,0:T(8,128)S(1)} async-done(((f32[32,2,96,128]{3,2,1,0:T(8,128)}), f32[32,2,96,128]{3,2,1,0:T(8,128)S(1)}, u32[]{:S(2)}, u32[]{:S(2)}) %all-to-all-start) | async-done | bytes 3145760 | tf_op jit(solution)/shard_map/all_to_all | solution.py:453
  79.4 6.2 %prior.1 = (f32[2,96,4096]{2,1,0:T(8,128)}, f32[32,2,96,128]{3,2,1,0:T(8,128)S(1)}) custom-call(f32[32,2,96,128]{3,2,1,0:T(8,128)S(1)} %all-to-all-done.refs_0_, f32[2,96,4096]{2,1,0:T(8,128)} %copy-done.1, f32[2,96,4096]{2,1,0:T(8,128)} %refs_2_.1, bf16[384,256]{1,0:T(8,128)(2,1)S(1)} %get-tuple-element.7.refs_3_, bf16[96,192]{1,0:T(8,128)(2,1)} %constant.42.clone.refs_4_, ...), custom_call_target="tpu_custom_call" | custom-call | tf_op jit(solution)/shard_map/prior/pallas_call | solution.py:392
  85.7 0.0 copy-start
  85.7 74.9 %all_to_all.10 = f32[32,2,96,128]{3,2,1,0:T(8,128)S(1)} all-to-all(f32[32,2,96,128]{3,2,1,0:T(8,128)S(1)} %get-tuple-element.9), channel_id=1, replica_groups=mesh['groups'=1,'fac'=32] {'fac'}, dimensions={0} | all-to-all | bytes 6291456 | tf_op jit(solution)/shard_map/all_to_all | solution.py:458
  160.6 0.0 copy-done
  160.6 2.5 %shrink.1 = f32[64,96,128]{2,1,0:T(8,128)} custom-call(f32[64,96,128]{2,1,0:T(8,128)S(1)} %copy-done, f32[64,96,128]{2,1,0:T(8,128)S(1)} %bitcast.9), custom_call_target="tpu_custom_call" | custom-call | tf_op jit(solution)/shard_map/shrink/pallas_call | solution.py:437
Async XLA Ops:
  0.6 78.8 %all-to-all-start = ((f32[32,2,96,128]{3,2,1,0:T(8,128)}), f32[32,2,96,128]{3,2,1,0:T(8,128)S(1)}, u32[]{:S(2)}, u32[]{:S(2)}) async-start(f32[32,2,96,128]{3,2,1,0:T(8,128)} %bitcast.8), calls=%async_computation | async-start | bytes 6291456 | tf_op jit(solution)/shard_map/all_to_all | solution.py:453
  64.7 1.7 %copy-start.1 = (f32[2,96,4096]{2,1,0:T(8,128)}, f32[2,96,4096]{2,1,0:T(8,128)S(1)}, u32[]{:S(2)}) copy-start(f32[2,96,4096]{2,1,0:T(8,128)S(1)} %get-tuple-element.6.refs_1_) | copy-start | bytes 9437188
  85.7 74.9 %copy-start = (f32[64,96,128]{2,1,0:T(8,128)S(1)}, f32[64,96,128]{2,1,0:T(8,128)}, u32[]{:S(2)}) copy-start(f32[64,96,128]{2,1,0:T(8,128)} %dual.1) | copy-start | bytes 9437188

commit v5 on v4

--- a/solution.py
+++ b/solution.py
@@ -439,7 +439,7 @@
         out_shape=jax.ShapeDtypeStruct(dual.shape, f32),
         in_specs=[resident, resident],
         out_specs=distant,
-        scratch_shapes=[pltpu.VMEM(dual.shape, f32), pltpu.SemaphoreType.DMA((8,))],
+        scratch_shapes=[pltpu.VMEM(dual.shape, f32), pltpu.SemaphoreType.DMA((16,))],
         compiler_params=pltpu.CompilerParams(vmem_limit_bytes=6 << 20),
         name="shrink",
     )(dual, change)

time: 164 us -> 164 us (level)
  no operation moved by 1% of the time
where the time goes in v5:
time: 164 us; the launch traced here: 163 us
  blocking collectives  74.9 us (46%)
  Pallas kernels  34.8 us (21%)
  local copies, waits for them, and re-layouts  32.4 us (20%)
  waiting for transfers between devices  13 us (8%)
  starting transfers between devices  7.3 us (4%)
    all_to_all x1, blocking collectives, shards(): lax.all_to_all(change, 'fac', split_axis=0, concat_axis=0, tiled=True)  74.9 us
    pallas_call x1, Pallas kernels, fidelity(): pl.pallas_call(fidelity_kernel, out_shape=(jax.ShapeDtypeStruct(sky.shape...  26 us
    unnamed x7, local copies, waits for them, and re-layouts  17 us
    reshape x3, local copies, waits for them, and re-layouts, by_slab(): return values.reshape(channels, rows, LANES, slabs).transpose(0, 3, 1, 2)  15.5 us
    all_to_all x1, waiting for transfers between devices, shards(): coefs = lax.all_to_all(sent, 'fac', split_axis=0, concat_axis=0, tiled=True)  13 us
    all_to_all x1, starting transfers between devices, shards(): coefs = lax.all_to_all(sent, 'fac', split_axis=0, concat_axis=0, tiled=True)  7.3 us
    pallas_call x1, Pallas kernels, prior(): pl.pallas_call(prior_kernel, out_shape=(jax.ShapeDtypeStruct(sky.shape, f...  6.25 us
  transfers between devices with their start and end apart: 1, of which 1 were waited for; matrix products, arithmetic and copies ran while one was open for 19% of the time, Pallas kernels for 16%

profile of v5, /device:TPU:0, one launch (start us, length us, event | category | flops | bytes accessed | tf_op | source)
XLA Modules:
  0.0 163.2 jit_solution(2459435217066702466)
XLA Ops:
  0.6 7.3 %all-to-all-start = ((f32[32,2,96,128]{3,2,1,0:T(8,128)}), f32[32,2,96,128]{3,2,1,0:T(8,128)S(1)}, u32[]{:S(2)}, u32[]{:S(2)}) async-start(f32[32,2,96,128]{3,2,1,0:T(8,128)} %bitcast.8), calls=%async_computation | async-start | bytes 6291456 | tf_op jit(solution)/shard_map/all_to_all | solution.py:453
  7.9 5.1 %copy.23 = f32[2,96,4096]{1,2,0:T(8,128)} copy(f32[2,96,4096]{2,1,0:T(8,128)} %param.22) | data formatting | bytes 6291456 | tf_op args[1]
  13.1 5.1 %copy.24 = f32[2,96,128,32]{2,1,3,0:T(8,128)} copy(f32[2,96,128,32]{1,3,2,0:T(8,128)} %bitcast.10) | data formatting | bytes 6291456 | tf_op jit(solution)/shard_map/reshape | solution.py:242
  18.2 5.1 %copy.25 = f32[2,96,4096]{1,2,0:T(8,128)} copy(f32[2,96,4096]{2,1,0:T(8,128)} %param.23) | data formatting | bytes 6291456 | tf_op args[2]
  23.3 5.1 %copy.26 = f32[2,96,128,32]{2,1,3,0:T(8,128)} copy(f32[2,96,128,32]{1,3,2,0:T(8,128)} %bitcast.11) | data formatting | bytes 6291456 | tf_op jit(solution)/shard_map/reshape | solution.py:242
  28.4 5.1 %copy.27 = s32[2,96,4096]{1,2,0:T(8,128)} copy(s32[2,96,4096]{2,1,0:T(8,128)} %param.24) | data formatting | bytes 6291456 | tf_op args[3]
  33.5 5.2 %copy.28 = s32[2,96,128,32]{2,1,3,0:T(8,128)} copy(s32[2,96,128,32]{1,3,2,0:T(8,128)} %bitcast.12) | data formatting | bytes 6291456 | tf_op jit(solution)/shard_map/reshape | solution.py:242
  38.7 26.0 %fidelity.1 = (f32[2,96,4096]{2,1,0:T(8,128)S(1)}, bf16[384,256]{1,0:T(8,128)(2,1)S(1)}) custom-call(f32[2,96,4096]{2,1,0:T(8,128)} %refs_2_.1, f32[2,32,96,128]{3,2,1,0:T(8,128)} %bitcast.13, f32[2,32,96,128]{3,2,1,0:T(8,128)} %bitcast.14, s32[2,32,96,128]{3,2,1,0:T(8,128)} %bitcast.15, bf16[192,96]{1,0:T(8,128)(2,1)} %constant.33.clone.row_hi, ...), custom_call_target="tpu_custom_call" | custom-call | tf_op jit(solution)/shard_map/fidelity/pallas_call | solution.py:253
  64.7 0.0 copy-start.1
  64.7 1.7 %copy-done.1 = f32[2,96,4096]{2,1,0:T(8,128)} copy-done((f32[2,96,4096]{2,1,0:T(8,128)}, f32[2,96,4096]{2,1,0:T(8,128)S(1)}, u32[]{:S(2)}) %copy-start.1) | copy-done | bytes 3145752
  66.4 13.0 %all-to-all-done.refs_0_ = f32[32,2,96,128]{3,2,1,0:T(8,128)S(1)} async-done(((f32[32,2,96,128]{3,2,1,0:T(8,128)}), f32[32,2,96,128]{3,2,1,0:T(8,128)S(1)}, u32[]{:S(2)}, u32[]{:S(2)}) %all-to-all-start) | async-done | bytes 3145760 | tf_op jit(solution)/shard_map/all_to_all | solution.py:453
  79.4 6.2 %prior.1 = (f32[2,96,4096]{2,1,0:T(8,128)}, f32[32,2,96,128]{3,2,1,0:T(8,128)S(1)}) custom-call(f32[32,2,96,128]{3,2,1,0:T(8,128)S(1)} %all-to-all-done.refs_0_, f32[2,96,4096]{2,1,0:T(8,128)} %copy-done.1, f32[2,96,4096]{2,1,0:T(8,128)} %refs_2_.1, bf16[384,256]{1,0:T(8,128)(2,1)S(1)} %get-tuple-element.7.refs_3_, bf16[96,192]{1,0:T(8,128)(2,1)} %constant.42.clone.refs_4_, ...), custom_call_target="tpu_custom_call" | custom-call | tf_op jit(solution)/shard_map/prior/pallas_call | solution.py:392
  85.7 0.0 copy-start
  85.7 74.9 %all_to_all.10 = f32[32,2,96,128]{3,2,1,0:T(8,128)S(1)} all-to-all(f32[32,2,96,128]{3,2,1,0:T(8,128)S(1)} %get-tuple-element.9), channel_id=1, replica_groups=mesh['groups'=1,'fac'=32] {'fac'}, dimensions={0} | all-to-all | bytes 6291456 | tf_op jit(solution)/shard_map/all_to_all | solution.py:458
  160.6 0.0 copy-done
  160.6 2.6 %shrink.1 = f32[64,96,128]{2,1,0:T(8,128)} custom-call(f32[64,96,128]{2,1,0:T(8,128)S(1)} %copy-done, f32[64,96,128]{2,1,0:T(8,128)S(1)} %bitcast.9), custom_call_target="tpu_custom_call" | custom-call | tf_op jit(solution)/shard_map/shrink/pallas_call | solution.py:437
Async XLA Ops:
  0.6 78.8 %all-to-all-start = ((f32[32,2,96,128]{3,2,1,0:T(8,128)}), f32[32,2,96,128]{3,2,1,0:T(8,128)S(1)}, u32[]{:S(2)}, u32[]{:S(2)}) async-start(f32[32,2,96,128]{3,2,1,0:T(8,128)} %bitcast.8), calls=%async_computation | async-start | bytes 6291456 | tf_op jit(solution)/shard_map/all_to_all | solution.py:453
  64.7 1.7 %copy-start.1 = (f32[2,96,4096]{2,1,0:T(8,128)}, f32[2,96,4096]{2,1,0:T(8,128)S(1)}, u32[]{:S(2)}) copy-start(f32[2,96,4096]{2,1,0:T(8,128)S(1)} %get-tuple-element.6.refs_1_) | copy-start | bytes 9437188
  85.7 74.9 %copy-start = (f32[64,96,128]{2,1,0:T(8,128)S(1)}, f32[64,96,128]{2,1,0:T(8,128)}, u32[]{:S(2)}) copy-start(f32[64,96,128]{2,1,0:T(8,128)} %dual.1) | copy-start | bytes 9437188
